TPU v7x, 32 devices: a whole 2x2x4 slice. The times are simulated.
32 devices in a mesh: row: 16 (over z, y, core), col: 2 (over x).
Axes of the slice: x: 2, y: 2, z: 4, core: 2. Of those that a mesh axis runs over, the one named last changes fastest.
Arguments:
- pair: bfloat16 [384, 384, 128], P('row', 'col'), may hold values from -6 to 6
- gain: float32 [128], replicated, may hold values from 0.1 to 1.9
- projections: bfloat16 [5, 128, 128], replicated, may hold values from -0.5 to 0.5
- bias_weight: bfloat16 [128, 4], replicated, as said below
- valid_len: int32 [1], replicated, may hold values from 192 to 384
- out_cotangent: bfloat16 [384, 384, 128], P('row', 'col'), may hold values from -6 to 6
Outputs:
- attended: bfloat16 [384, 384, 128], P('row', 'col')
- pair_gradient: float32 [384, 384, 128], P('row', 'col')
- projection_grad: float32 [5, 128, 128], replicated
- bias_weight_grad: float32 [128, 4], replicated
- gain_gradient: float32 [128], replicated
Inputs may be any that keep to these rules, and one draw needn't show every extreme that they name: `bias_weight`: scale of the bias projection entries is free; rows are drawn independently.
All inputs are finite; a program needn't handle non-finite values.
Results may differ from a plain program's by a relative error of at most 0.0045.
The roundings to bfloat16 on the way count: a program that leaves them out, or rounds other values in their place, can miss the bound.
Values may be sent and summed in bfloat16 or wider, within the bound.
A program may use at most 64 MiB of HBM per device.

v0:
```python
import functools

import jax
import jax.numpy as jnp
from jax import lax
from jax.experimental import pallas as pl
from jax.experimental.pallas import tpu as pltpu
from jax.sharding import PartitionSpec as P

EPS = 1e-05
F32 = jnp.float32
BF16 = jnp.bfloat16


def mm(left, right):
    return lax.dot_general(left, right, (((1,), (0,)), ((), ())), preferred_element_type=F32)


def mm_nt(left, right):
    return lax.dot_general(left, right, (((1,), (1,)), ((), ())), preferred_element_type=F32)


def attention_kernel(
    heads, valid_ref, x_ref, cot_ref, w_in_ref, w_out_ref, bias_ref,
    att_ref, dn_ref, dbias_ref, parts_ref, bias_s, dbias_s,
):
    step = pl.program_id(0)
    n_row, _, tile_rows, channels = x_ref.shape
    n_col, tile_cols = bias_ref.shape[1], bias_ref.shape[4]
    rows = n_row * tile_rows
    width = channels // heads
    scale = width ** (-0.5)
    keep_lanes = lax.broadcasted_iota(jnp.int32, (rows, 1), 0) < valid_ref[0]

    @pl.when(step == 0)
    def _():
        for h in range(heads):
            for c in range(n_col):
                block = bias_ref[:, c, h].reshape(rows, tile_cols)
                bias_s[h, :, c * tile_cols : (c + 1) * tile_cols] = jnp.where(
                    keep_lanes, block, -1000000000.0
                )
        dbias_s[...] = jnp.zeros_like(dbias_s)
        parts_ref[...] = jnp.zeros_like(parts_ref)

    x = x_ref[:, 0].astype(F32).reshape(rows, channels).astype(BF16)
    cot = cot_ref[:, 0].astype(F32).reshape(rows, channels).astype(BF16)
    proj = mm(x, w_in_ref[...])
    query = proj[:, :channels].astype(BF16)
    key_f = jnp.where(keep_lanes, proj[:, channels : 2 * channels], 0.0)
    key = key_f.astype(BF16)
    value_f = proj[:, 2 * channels : 3 * channels]
    value = value_f.astype(BF16)
    gate = jax.nn.sigmoid(proj[:, 3 * channels :])
    d_gated = mm_nt(cot, w_out_ref[...])
    d_context_f = d_gated * gate
    d_context = d_context_f.astype(BF16)
    key_t = jnp.transpose(key_f).astype(BF16)
    value_t = jnp.transpose(value_f).astype(BF16)
    lane_head = lax.broadcasted_iota(jnp.int32, (rows, channels), 1) // width
    ctx_parts, dq_parts = [], []
    dk = jnp.zeros((rows, channels), F32)
    dv = jnp.zeros((rows, channels), F32)
    for h in range(heads):
        mine = lane_head == h
        q_h = jnp.where(mine, query, jnp.zeros_like(query))
        dc_h = jnp.where(mine, d_context, jnp.zeros_like(d_context))
        s = mm_nt(key, q_h) * scale + bias_s[h]
        e = jnp.exp(s - jnp.max(s, axis=0, keepdims=True))
        p = e * (1.0 / jnp.sum(e, axis=0, keepdims=True))
        d_p = mm_nt(value, dc_h)
        delta = jnp.sum(p * d_p, axis=0, keepdims=True)
        ds = p * (d_p - delta)
        dbias_s[h] += ds
        p_b = p.astype(BF16)
        ds_b = ds.astype(BF16)
        ctx_parts.append(mm(value_t[h * width : (h + 1) * width], p_b))
        dq_parts.append(mm(key_t[h * width : (h + 1) * width], ds_b))
        dv += mm(p_b, dc_h)
        dk += mm(ds_b, q_h)
    context = jnp.transpose(jnp.concatenate(ctx_parts, axis=0)).astype(BF16).astype(F32)
    dq = (jnp.transpose(jnp.concatenate(dq_parts, axis=0)) * scale).astype(BF16)
    dk = (dk * scale).astype(BF16)
    dv = dv.astype(BF16)
    gated_f = gate * context
    gated = gated_f.astype(BF16)
    att = mm(gated, w_out_ref[...])
    att_ref[:, 0] = att.reshape(n_row, tile_rows, channels).astype(att_ref.dtype)
    d_gate = (d_gated * context * gate * (1.0 - gate)).astype(BF16)
    grads = jnp.concatenate([dq, dk, dv, d_gate], axis=1)
    dn = mm_nt(grads, w_in_ref[...])
    dn_ref[:, 0] = dn.reshape(n_row, tile_rows, channels).astype(dn_ref.dtype)
    x_t = jnp.transpose(x.astype(F32)).astype(BF16)
    parts_ref[:, : 4 * channels] += mm(x_t, grads)
    gated_t = jnp.transpose(gated.astype(F32)).astype(BF16)
    parts_ref[:, 4 * channels :] += mm(gated_t, cot)

    @pl.when(step == pl.num_programs(0) - 1)
    def _():
        for h in range(heads):
            for c in range(n_col):
                block = dbias_s[h, :, c * tile_cols : (c + 1) * tile_cols]
                dbias_ref[:, c, h] = block.reshape(n_row, tile_rows, tile_cols).astype(dbias_ref.dtype)


def attention(valid_len, x_cols, cot_cols, w_in, w_out, bias):
    n_row, ncols, tile_rows, channels = x_cols.shape
    heads, n_col, tile_cols = bias.shape[2], bias.shape[1], bias.shape[4]
    rows = n_row * tile_rows
    column = pl.BlockSpec((n_row, 1, tile_rows, channels), lambda j: (0, j, 0, 0))

    def whole(shape):
        return pl.BlockSpec(shape, lambda j: (0,) * len(shape))

    return pl.pallas_call(
        functools.partial(attention_kernel, heads),
        grid=(ncols,),
        in_specs=[
            pl.BlockSpec(memory_space=pltpu.SMEM),
            column,
            column,
            whole(w_in.shape),
            whole(w_out.shape),
            whole(bias.shape),
        ],
        out_specs=[column, column, whole(bias.shape), whole((channels, 5 * channels))],
        out_shape=[
            jax.ShapeDtypeStruct(x_cols.shape, BF16),
            jax.ShapeDtypeStruct(x_cols.shape, BF16),
            jax.ShapeDtypeStruct(bias.shape, BF16),
            jax.ShapeDtypeStruct((channels, 5 * channels), F32),
        ],
        scratch_shapes=[
            pltpu.VMEM((heads, rows, rows), F32),
            pltpu.VMEM((heads, rows, rows), F32),
        ],
        compiler_params=pltpu.CompilerParams(
            dimension_semantics=("arbitrary",), vmem_limit_bytes=60 * 1024 * 1024
        ),
    )(valid_len, x_cols, cot_cols, w_in, w_out, bias)


def shards(pair, gain, projections, bias_weight, valid_len, out_cotangent):
    n_row = lax.axis_size("row")
    n_col = lax.axis_size("col")
    tile_rows, tile_cols, channels = pair.shape
    heads = bias_weight.shape[1]
    ncols = tile_cols // n_row
    pair_float = pair.astype(F32)
    average_value = jnp.mean(pair_float, axis=-1, keepdims=True)
    var = jnp.mean((pair_float - average_value) ** 2, axis=-1, keepdims=True)
    inverse_deviation = lax.rsqrt(var + EPS)
    centered_scaled = (pair_float - average_value) * inverse_deviation
    normalized_pair = (centered_scaled * gain).astype(BF16)
    bias_tile = jnp.einsum("abc,ch->hab", normalized_pair, bias_weight, preferred_element_type=F32)
    gathered = lax.all_gather(bias_tile[None], ("row", "col"), axis=0, tiled=True)
    gathered = gathered.reshape(n_row, n_col, heads, tile_rows, tile_cols)

    def to_columns(tile):
        moved = jnp.swapaxes(tile, 0, 1).reshape(n_row, ncols, tile_rows, channels)
        return lax.all_to_all(moved, "row", split_axis=0, concat_axis=0, tiled=True)

    def to_tile(columns):
        moved = lax.all_to_all(columns, "row", split_axis=0, concat_axis=0, tiled=True)
        return jnp.swapaxes(moved.reshape(tile_cols, tile_rows, channels), 0, 1)

    x_cols, cot_cols = to_columns(normalized_pair), to_columns(out_cotangent)
    w_in = jnp.swapaxes(projections[:4], 0, 1).reshape(channels, 4 * channels)
    att_cols, dn_cols, total, parts = attention(
        valid_len, x_cols, cot_cols, w_in, projections[4], gathered
    )
    everyone = ("row", "col")
    n_all = n_row * n_col

    def swap(blocks):
        return lax.all_to_all(blocks, everyone, split_axis=0, concat_axis=0, tiled=True)

    shares = swap(total.reshape(n_all, heads, tile_rows, tile_cols))
    d_bias = jnp.sum(shares.astype(F32), axis=0).astype(BF16)
    parts = jnp.swapaxes(parts.reshape(channels, 5, channels), 0, 1)
    slab = 5 * channels // n_all
    owned = jnp.sum(swap(parts.reshape(n_all, slab, channels)), axis=0)
    attended = to_tile(att_cols)
    bias_term = jnp.einsum("hab,ch->abc", d_bias, bias_weight, preferred_element_type=F32)
    bias_weight_part = jnp.einsum(
        "hab,abc->hc", d_bias, normalized_pair, preferred_element_type=F32
    )
    normalized_gradient = to_tile(dn_cols).astype(F32) + bias_term
    gain_partial_sum = jnp.sum(normalized_gradient * centered_scaled, axis=(0, 1))
    mine = jnp.concatenate([owned, bias_weight_part, gain_partial_sum[None]], axis=0)
    spread = swap(jnp.broadcast_to(mine[None], (n_all,) + mine.shape))
    projection_grad = spread[:, :slab].reshape(5, channels, channels)
    small = jnp.sum(spread[:, slab:], axis=0)
    bias_weight_grad, gain_gradient = small[:heads].T, small[heads]
    scaled_output = normalized_gradient * gain
    pair_gradient = inverse_deviation * (
        scaled_output
        - jnp.mean(scaled_output, axis=-1, keepdims=True)
        - centered_scaled * jnp.mean(scaled_output * centered_scaled, axis=-1, keepdims=True)
    )
    return (attended, pair_gradient, projection_grad, bias_weight_grad, gain_gradient)


def solution(mesh):
    placed = (P("row", "col", None), P(), P(), P(), P(), P("row", "col", None))
    return jax.shard_map(
        shards,
        mesh=mesh,
        in_specs=placed,
        out_specs=(P("row", "col", None), P("row", "col", None), P(), P(), P()),
        check_vma=False,
    )
```

profile of v0, /device:TPU:0, one launch (start us, length us, event | category | flops | bytes accessed | tf_op | source)
XLA Modules:
  0.0 301.9 jit_solution(8153789767810938277)
XLA Ops:
  7.2 0.0 copy-start
  7.2 0.0 copy-start.1
  7.2 0.0 copy-start.18
  7.2 0.0 all-gather.3.cloned.1.call-start
  7.2 1.8 convert_reduce_fusion
  9.1 2.8 fusion.11
  12.0 2.0 convolution_bitcast_fusion
  14.0 0.7 copy.28
  14.6 0.0 all-gather.3.cloned.1.call-update
  14.6 1.5 fusion.14
  16.1 0.0 copy-start.5
  16.1 1.8 copy.25
  17.9 7.4 %all-to-all-start = ((bf16[16,12,24,128]{3,2,1,0:T(8,128)(2,1)}), bf16[16,12,24,128]{3,2,1,0:T(8,128)(2,1)S(1)}, u32[]{:S(2)}, u32[]{:S(2)}) async-start(bf16[16,12,24,128]{3,2,1,0:T(8,128)(2,1)} %bitcast.1), calls=%async_computation | async-start | bytes 2359296 | tf_op jit(solution)/shard_map/all_to_all | solution.py:161
  25.3 1.8 copy.26
  27.1 25.3 %all-to-all-done.x_ref = bf16[16,12,24,128]{3,2,1,0:T(8,128)(2,1)S(1)} async-done(((bf16[16,12,24,128]{3,2,1,0:T(8,128)(2,1)}), bf16[16,12,24,128]{3,2,1,0:T(8,128)(2,1)S(1)}, u32[]{:S(2)}, u32[]{:S(2)}) %all-to-all-start) | async-done | bytes 1179680 | tf_op jit(solution)/shard_map/all_to_all | solution.py:161
  52.4 8.9 %all-to-all-start.1 = ((bf16[16,12,24,128]{3,2,1,0:T(8,128)(2,1)}), bf16[16,12,24,128]{3,2,1,0:T(8,128)(2,1)S(1)}, u32[]{:S(2)}, u32[]{:S(2)}) async-start(bf16[16,12,24,128]{3,2,1,0:T(8,128)(2,1)} %bitcast.3), calls=%async_computation.1 | async-start | bytes 2359296 | tf_op jit(solution)/shard_map/all_to_all | solution.py:161
  62.0 1.4 slice_bitcast_fusion.1.w_out_ref
  63.4 1.6 copy_bitcast_fusion.1.w_in_ref
  64.9 30.1 %all-to-all-done.1.cot_ref = bf16[16,12,24,128]{3,2,1,0:T(8,128)(2,1)S(1)} async-done(((bf16[16,12,24,128]{3,2,1,0:T(8,128)(2,1)}), bf16[16,12,24,128]{3,2,1,0:T(8,128)(2,1)S(1)}, u32[]{:S(2)}, u32[]{:S(2)}) %all-to-all-start.1) | async-done | bytes 1179680 | tf_op jit(solution)/shard_map/all_to_all | solution.py:161
  95.1 1.0 copy-done.3
  96.1 46.4 %shard_map.101 = (bf16[16,12,24,128]{3,2,1,0:T(8,128)(2,1)}, bf16[16,12,24,128]{3,2,1,0:T(8,128)(2,1)}, bf16[16,2,4,24,192]{4,3,2,1,0:T(8,128)(2,1)}, f32[128,640]{1,0:T(8,128)}) custom-call(s32[1]{0:T(128)S(6)} %copy.46.valid_ref, bf16[16,12,24,128]{3,2,1,0:T(8,128)(2,1)} %copy-done.2, bf16[16,12,24,128]{3,2,1,0:T(8,128)(2,1)} %copy-done.3, ...), custom_call_target="tpu_custom_call" | custom-call | tf_op jit(solution)/shard_map/pallas_call | solution.py:115
  142.5 1.2 copy.32
  143.8 0.2 copy.33
  144.0 20.2 %all_to_all.35 = f32[32,20,128]{2,1,0:T(8,128)S(1)} all-to-all(f32[32,20,128]{2,1,0:T(8,128)S(1)} %reshape.69), channel_id=1, replica_groups=mesh['row'=16,'col'=2] {'row','col'}, dimensions={0} | all-to-all | bytes 655360 | tf_op jit(solution)/shard_map/all_to_all | solution.py:176
  164.1 32.8 %all_to_all.36 = bf16[16,12,24,128]{3,2,1,0:T(8,128)(2,1)} all-to-all(bf16[16,12,24,128]{3,2,1,0:T(8,128)(2,1)S(1)} %copy-done.6), channel_id=1, replica_groups=mesh['row'=16,'col'=2] {'row'}, dimensions={0} | all-to-all | bytes 2359296 | tf_op jit(solution)/shard_map/all_to_all | solution.py:164
  196.9 40.4 %all_to_all.37 = bf16[32,4,24,192]{3,2,1,0:T(8,128)(2,1)S(1)} all-to-all(bf16[32,4,24,192]{3,2,1,0:T(8,128)(2,1)} %bitcast.44), channel_id=1, replica_groups=mesh['row'=16,'col'=2] {'row','col'}, dimensions={0} | all-to-all | bytes 2359296 | tf_op jit(solution)/shard_map/all_to_all | solution.py:176
  237.3 4.6 %all-to-all-start.2 = ((bf16[16,12,24,128]{3,2,1,0:T(8,128)(2,1)}), bf16[16,12,24,128]{3,2,1,0:T(8,128)(2,1)}, u32[]{:S(2)}, u32[]{:S(2)}) async-start(bf16[16,12,24,128]{3,2,1,0:T(8,128)(2,1)} %get-tuple-element.9), calls=%async_computation.2 | async-start | bytes 2359296 | tf_op jit(solution)/shard_map/all_to_all | solution.py:164
  242.0 0.0 copy-start.19
  242.0 2.8 bitcast_convert_fusion
  244.8 0.3 reduce_sum.77
  245.1 0.0 copy-start.15
  245.1 0.6 copy-done.15
  245.8 0.0 copy-start.20
  245.8 1.8 convolution_bitcast_fusion.1
  247.6 5.6 %fusion.10 = (f32[128]{0:T(128)S(1)}, f32[24,192]{1,0:T(8,128)}, f32[24,192]{1,0:T(8,128)}, f32[24,192,128]{2,1,0:T(8,128)S(1)}) fusion(bf16[24,192,128]{2,1,0:T(8,128)(2,1)S(1)} %copy-done.1, f32[24,192]{1,0:T(8,128)S(1)} %copy-done.13, f32[24,192]{1,0:T(8,128)S(1)} %copy-done.9, f32[128]{0:T(128)S(1)} %copy-done.20, bf16[128,4]{0,1:T(4,128)(2,1)S(1)} %copy-done, ...), kind=kOutput, calls=%fused_computation.12 | convolution fusion | flops 10607488 | bytes 6010880 | tf_op jit(solution)/shard_map/hab,ch->abc/dot_general | solution.py:184
  253.2 0.6 pad_maximum_fusion
  253.8 12.9 %all-to-all-done.2 = bf16[16,12,24,128]{3,2,1,0:T(8,128)(2,1)} async-done(((bf16[16,12,24,128]{3,2,1,0:T(8,128)(2,1)}), bf16[16,12,24,128]{3,2,1,0:T(8,128)(2,1)}, u32[]{:S(2)}, u32[]{:S(2)}) %all-to-all-start.2) | async-done | bytes 1179680 | tf_op jit(solution)/shard_map/all_to_all | solution.py:164
  266.8 1.6 broadcast_in_dim.8
  268.4 7.8 %all-to-all-start.6 = ((f32[32,25,128]{2,1,0:T(8,128)}), f32[32,25,128]{2,1,0:T(8,128)}, u32[]{:S(2)}, u32[]{:S(2)}) async-start(f32[32,25,128]{2,1,0:T(8,128)} %broadcast_in_dim.8), calls=%async_computation.6 | async-start | bytes 1048576 | tf_op jit(solution)/shard_map/all_to_all | solution.py:176
  276.2 0.0 copy-start.16
  276.2 2.6 copy.45
  278.8 5.4 %fusion.9 = f32[24,192,128]{2,1,0:T(8,128)} fusion(bf16[24,192,128]{2,1,0:T(8,128)(2,1)S(1)} %copy-done.1, f32[24,192,128]{2,1,0:T(8,128)S(1)} %get-tuple-element.16, f32[24,192]{1,0:T(8,128)S(1)} %get-tuple-element.17, f32[24,192]{1,0:T(8,128)S(1)} %get-tuple-element.18, f32[128]{0:T(128)} %param.7, f32[24,192]{1,0:T(8,128)S(1)} %copy-done.14, ...), kind=kLoop, calls=%fused_computation.11 | loop fusion | flops 4718592 | bytes 5972480 | tf_op jit(solution)/shard_map/mul | solution.py:196
  284.3 6.9 %all-to-all-done.6 = f32[32,25,128]{2,1,0:T(8,128)} async-done(((f32[32,25,128]{2,1,0:T(8,128)}), f32[32,25,128]{2,1,0:T(8,128)}, u32[]{:S(2)}, u32[]{:S(2)}) %all-to-all-start.6) | async-done | bytes 409632 | tf_op jit(solution)/shard_map/all_to_all | solution.py:176
  291.1 1.0 slice_reduce_fusion
  292.1 0.5 slice_bitcast_fusion.3
  292.7 0.6 slice_bitcast_fusion.2
  293.2 1.0 slice.24
  294.3 0.8 reshape.70
  (38 shorter events, 0.2 us)
Async XLA Ops:
  7.2 4.8 %copy-start = (bf16[128,4]{0,1:T(4,128)(2,1)S(1)}, bf16[128,4]{0,1:T(4,128)(2,1)}, u32[]{:S(2)}) copy-start(bf16[128,4]{0,1:T(4,128)(2,1)} %param.9) | copy-start | bytes 3076
  7.2 4.8 %copy-start.1 = (bf16[24,192,128]{2,1,0:T(8,128)(2,1)S(1)}, bf16[24,192,128]{2,1,0:T(8,128)(2,1)}, u32[]{:S(2)}) copy-start(bf16[24,192,128]{2,1,0:T(8,128)(2,1)} %param.6) | copy-start | bytes 3538948
  7.2 4.8 %copy-start.18 = (f32[128]{0:T(128)S(1)}, f32[128]{0:T(128)}, u32[]{:S(2)}) copy-start(f32[128]{0:T(128)} %param.7) | copy-start | bytes 1540
  7.2 87.9 %all-gather.3.cloned.1.call-start = ((), (), s32[]{:S(2)}) async-start(), calls=%async_computation.7 | async-start | bytes 3244032 | tf_op jit(solution)/shard_map/all_gather | solution.py:156
  9.1 7.0 %copy-start.7 = (f32[24,192]{1,0:T(8,128)}, f32[24,192]{1,0:T(8,128)S(1)}, u32[]{:S(2)}) copy-start(f32[24,192]{1,0:T(8,128)S(1)} %broadcast_multiply_fusion.2) | copy-start | bytes 55300
  12.0 4.2 %copy-start.11 = (f32[24,192]{1,0:T(8,128)}, f32[24,192]{1,0:T(8,128)S(1)}, u32[]{:S(2)}) copy-start(f32[24,192]{1,0:T(8,128)S(1)} %add_rsqrt_fusion) | copy-start | bytes 55300
  16.1 9.2 %copy-start.5 = (bf16[24,192,128]{2,1,0:T(8,128)(2,1)S(1)}, bf16[24,192,128]{2,1,0:T(8,128)(2,1)}, u32[]{:S(2)}) copy-start(bf16[24,192,128]{2,1,0:T(8,128)(2,1)} %param.11) | copy-start | bytes 3538948
  17.9 34.5 %all-to-all-start = ((bf16[16,12,24,128]{3,2,1,0:T(8,128)(2,1)}), bf16[16,12,24,128]{3,2,1,0:T(8,128)(2,1)S(1)}, u32[]{:S(2)}, u32[]{:S(2)}) async-start(bf16[16,12,24,128]{3,2,1,0:T(8,128)(2,1)} %bitcast.1), calls=%async_computation | async-start | bytes 2359296 | tf_op jit(solution)/shard_map/all_to_all | solution.py:161
  52.4 42.7 %copy-start.2 = (bf16[16,12,24,128]{3,2,1,0:T(8,128)(2,1)}, bf16[16,12,24,128]{3,2,1,0:T(8,128)(2,1)S(1)}, u32[]{:S(2)}) copy-start(bf16[16,12,24,128]{3,2,1,0:T(8,128)(2,1)S(1)} %all-to-all-done.x_ref) | copy-start | bytes 3538948
  52.4 42.7 %all-to-all-start.1 = ((bf16[16,12,24,128]{3,2,1,0:T(8,128)(2,1)}), bf16[16,12,24,128]{3,2,1,0:T(8,128)(2,1)S(1)}, u32[]{:S(2)}, u32[]{:S(2)}) async-start(bf16[16,12,24,128]{3,2,1,0:T(8,128)(2,1)} %bitcast.3), calls=%async_computation.1 | async-start | bytes 2359296 | tf_op jit(solution)/shard_map/all_to_all | solution.py:161
  95.1 1.0 copy-start.3
  142.5 21.6 %copy-start.6 = (bf16[16,12,24,128]{3,2,1,0:T(8,128)(2,1)S(1)}, bf16[16,12,24,128]{3,2,1,0:T(8,128)(2,1)}, u32[]{:S(2)}) copy-start(bf16[16,12,24,128]{3,2,1,0:T(8,128)(2,1)} %get-tuple-element.10) | copy-start | bytes 3538948
  237.3 29.4 %all-to-all-start.2 = ((bf16[16,12,24,128]{3,2,1,0:T(8,128)(2,1)}), bf16[16,12,24,128]{3,2,1,0:T(8,128)(2,1)}, u32[]{:S(2)}, u32[]{:S(2)}) async-start(bf16[16,12,24,128]{3,2,1,0:T(8,128)(2,1)} %get-tuple-element.9), calls=%async_computation.2 | async-start | bytes 2359296 | tf_op jit(solution)/shard_map/all_to_all | solution.py:164
  242.0 3.8 %copy-start.8 = (f32[24,192]{1,0:T(8,128)S(1)}, f32[24,192]{1,0:T(8,128)}, u32[]{:S(2)}) copy-start(f32[24,192]{1,0:T(8,128)} %copy-done.7) | copy-start | bytes 55300
  242.0 3.8 %copy-start.12 = (f32[24,192]{1,0:T(8,128)S(1)}, f32[24,192]{1,0:T(8,128)}, u32[]{:S(2)}) copy-start(f32[24,192]{1,0:T(8,128)} %copy-done.11) | copy-start | bytes 55300
  242.0 3.8 %copy-start.19 = (f32[128]{0:T(128)S(1)}, f32[128]{0:T(128)}, u32[]{:S(2)}) copy-start(f32[128]{0:T(128)} %param.7) | copy-start | bytes 1540
  245.1 0.6 copy-start.15
  245.7 1.9 copy-start.4
  245.7 1.9 copy-start.9
  245.8 1.9 copy-start.13
  245.8 1.8 copy-start.20
  268.4 22.8 %all-to-all-start.6 = ((f32[32,25,128]{2,1,0:T(8,128)}), f32[32,25,128]{2,1,0:T(8,128)}, u32[]{:S(2)}, u32[]{:S(2)}) async-start(f32[32,25,128]{2,1,0:T(8,128)} %broadcast_in_dim.8), calls=%async_computation.6 | async-start | bytes 1048576 | tf_op jit(solution)/shard_map/all_to_all | solution.py:176
  276.2 2.6 copy-start.16
  276.2 2.6 copy-start.17
  276.2 2.6 copy-start.10
  276.2 2.6 copy-start.14
Sparse Core Ops, SparseCore 0:
  14.8 80.0 all-gather.2
where the time goes:
time: 303 us; the launch traced here: 302 us
  blocking collectives  93.4 us (31%)
  waiting for transfers between devices  75.2 us (25%)
  Pallas kernels  46.4 us (15%)
  starting transfers between devices  28.8 us (10%)
  local copies, waits for them, and re-layouts  17.4 us (6%)
  other arithmetic  16.3 us (5%)
  between operations  15 us (5%)
  matrix products  9.42 us (3%)
    all_to_all x2, blocking collectives, swap(): lax.all_to_all(blocks, everyone, split_axis=0, concat_axis=0, tiled=True)  60.6 us
    all_to_all x2, waiting for transfers between devices, to_columns(): return lax.all_to_all(moved, 'row', split_axis=0, concat_axis=0, tiled=True)  55.4 us
    pallas_call x1, Pallas kernels, attention(): pl.pallas_call(functools.partial(attention_kernel, heads), grid=(ncols,),...  46.4 us
    all_to_all x1, blocking collectives, to_tile(): lax.all_to_all(columns, 'row', split_axis=0, concat_axis=0, tiled=True)  32.8 us
    all_to_all x2, starting transfers between devices, to_columns(): return lax.all_to_all(moved, 'row', split_axis=0, concat_axis=0, tiled=True)  16.4 us
    all_to_all x1, waiting for transfers between devices, to_tile(): lax.all_to_all(columns, 'row', split_axis=0, concat_axis=0, tiled=True)  12.9 us
    all_to_all x1, starting transfers between devices, swap(): lax.all_to_all(blocks, everyone, split_axis=0, concat_axis=0, tiled=True)  7.8 us
    all_to_all x1, waiting for transfers between devices, swap(): lax.all_to_all(blocks, everyone, split_axis=0, concat_axis=0, tiled=True)  6.89 us
  transfers between devices with their start and end apart: 5, of which 4 were waited for; matrix products, arithmetic and copies ran while one was open for 9% of the time, Pallas kernels for 0%

commit v1 on v0

--- a/solution.py
+++ b/solution.py
@@ -25,7 +25,7 @@
     att_ref, dn_ref, dbias_ref, parts_ref, bias_s, dbias_s,
 ):
     step = pl.program_id(0)
-    n_row, _, tile_rows, channels = x_ref.shape
+    _, n_row, tile_rows, channels = x_ref.shape
     n_col, tile_cols = bias_ref.shape[1], bias_ref.shape[4]
     rows = n_row * tile_rows
     width = channels // heads
@@ -43,8 +43,8 @@
         dbias_s[...] = jnp.zeros_like(dbias_s)
         parts_ref[...] = jnp.zeros_like(parts_ref)
 
-    x = x_ref[:, 0].astype(F32).reshape(rows, channels).astype(BF16)
-    cot = cot_ref[:, 0].astype(F32).reshape(rows, channels).astype(BF16)
+    x = x_ref[0].astype(F32).reshape(rows, channels).astype(BF16)
+    cot = cot_ref[0].astype(F32).reshape(rows, channels).astype(BF16)
     proj = mm(x, w_in_ref[...])
     query = proj[:, :channels].astype(BF16)
     key_f = jnp.where(keep_lanes, proj[:, channels : 2 * channels], 0.0)
@@ -85,11 +85,11 @@
     gated_f = gate * context
     gated = gated_f.astype(BF16)
     att = mm(gated, w_out_ref[...])
-    att_ref[:, 0] = att.reshape(n_row, tile_rows, channels).astype(att_ref.dtype)
+    att_ref[0] = att.reshape(n_row, tile_rows, channels).astype(att_ref.dtype)
     d_gate = (d_gated * context * gate * (1.0 - gate)).astype(BF16)
     grads = jnp.concatenate([dq, dk, dv, d_gate], axis=1)
     dn = mm_nt(grads, w_in_ref[...])
-    dn_ref[:, 0] = dn.reshape(n_row, tile_rows, channels).astype(dn_ref.dtype)
+    dn_ref[0] = dn.reshape(n_row, tile_rows, channels).astype(dn_ref.dtype)
     x_t = jnp.transpose(x.astype(F32)).astype(BF16)
     parts_ref[:, : 4 * channels] += mm(x_t, grads)
     gated_t = jnp.transpose(gated.astype(F32)).astype(BF16)
@@ -100,14 +100,14 @@
         for h in range(heads):
             for c in range(n_col):
                 block = dbias_s[h, :, c * tile_cols : (c + 1) * tile_cols]
-                dbias_ref[:, c, h] = block.reshape(n_row, tile_rows, tile_cols).astype(dbias_ref.dtype)
+                dbias_ref[:, c, h] = block.reshape(n_row, tile_rows, tile_cols)
 
 
 def attention(valid_len, x_cols, cot_cols, w_in, w_out, bias):
-    n_row, ncols, tile_rows, channels = x_cols.shape
+    ncols, n_row, tile_rows, channels = x_cols.shape
     heads, n_col, tile_cols = bias.shape[2], bias.shape[1], bias.shape[4]
     rows = n_row * tile_rows
-    column = pl.BlockSpec((n_row, 1, tile_rows, channels), lambda j: (0, j, 0, 0))
+    column = pl.BlockSpec((1, n_row, tile_rows, channels), lambda j: (j, 0, 0, 0))
 
     def whole(shape):
         return pl.BlockSpec(shape, lambda j: (0,) * len(shape))
@@ -127,7 +127,7 @@
         out_shape=[
             jax.ShapeDtypeStruct(x_cols.shape, BF16),
             jax.ShapeDtypeStruct(x_cols.shape, BF16),
-            jax.ShapeDtypeStruct(bias.shape, BF16),
+            jax.ShapeDtypeStruct(bias.shape, F32),
             jax.ShapeDtypeStruct((channels, 5 * channels), F32),
         ],
         scratch_shapes=[
@@ -138,6 +138,273 @@
             dimension_semantics=("arbitrary",), vmem_limit_bytes=60 * 1024 * 1024
         ),
     )(valid_len, x_cols, cot_cols, w_in, w_out, bias)
+
+
+MESH = pl.DeviceIdType.MESH
+VM = pltpu.VMEM
+DMA = pltpu.SemaphoreType.DMA
+
+
+def place():
+    row, col = lax.axis_index("row"), lax.axis_index("col")
+    return row, col, row // 4, lax.rem(row // 2, 2), lax.rem(row, 2)
+
+
+def meet_all():
+    row, col = lax.axis_index("row"), lax.axis_index("col")
+    n_row, n_col = lax.axis_size("row"), lax.axis_size("col")
+    barrier = pltpu.get_barrier_semaphore()
+
+    def greet(i, carry):
+        there = (lax.rem(row + i // n_col, n_row), lax.rem(col + lax.rem(i, n_col), n_col))
+        pl.semaphore_signal(barrier, inc=1, device_id=there, device_id_type=MESH)
+        return carry
+
+    lax.fori_loop(1, n_row * n_col, greet, 0)
+    pl.semaphore_wait(barrier, n_row * n_col - 1)
+
+
+def push(src, dst, send, recv, where):
+    pltpu.make_async_remote_copy(
+        src_ref=src, dst_ref=dst, send_sem=send, recv_sem=recv,
+        device_id=where, device_id_type=MESH,
+    ).start()
+
+
+def await_bytes(ref, sem):
+    pltpu.make_async_copy(ref, ref, sem).wait()
+
+
+def mates(n_col, mid, col):
+    for i in range(1, 2 * n_col):
+        yield i - 1, lax.rem(mid + i // n_col, 2), lax.rem(col + i % n_col, n_col)
+
+
+def gather_kernel(
+    x_ref, cot_ref, bias_ref, xo_ref, coto_ref, biaso_ref,
+    s_aa, r_aa, s_out, r_out, s_mate, r_mate, s_core, r_core, s_loc,
+):
+    row, col, outer, mid, core = place()
+    n_row, ncols = x_ref.shape[:2]
+    n_out, _, _, n_col = biaso_ref.shape[:4]
+    meet_all()
+    for i in range(1, n_out):
+        there = lax.rem(outer + i, n_out) * 4 + mid * 2 + core
+        push(bias_ref, biaso_ref.at[outer, mid, core, col], s_out.at[i - 1], r_out.at[i - 1], (there, col))
+    local = [
+        pltpu.make_async_copy(bias_ref, biaso_ref.at[outer, mid, core, col], s_loc.at[0]),
+        pltpu.make_async_copy(x_ref.at[row], xo_ref.at[:, row], s_loc.at[1]),
+        pltpu.make_async_copy(cot_ref.at[row], coto_ref.at[:, row], s_loc.at[2]),
+    ]
+    for copy in local:
+        copy.start()
+
+    def columns(c, carry):
+        def peer(i, carry):
+            r = lax.rem(row + i, n_row)
+            push(x_ref.at[r, c], xo_ref.at[c, row], s_aa.at[0], r_aa.at[0, c], (r, col))
+            push(cot_ref.at[r, c], coto_ref.at[c, row], s_aa.at[1], r_aa.at[1, c], (r, col))
+            return carry
+
+        return lax.fori_loop(1, n_row, peer, carry)
+
+    split = (ncols + 1) // 2
+    lax.fori_loop(0, split, columns, 0)
+    for copy in local:
+        copy.wait()
+    for i in range(1, n_out):
+        await_bytes(bias_ref, s_out.at[i - 1])
+        await_bytes(bias_ref, r_out.at[i - 1])
+    mine = biaso_ref.at[:, mid, core, col]
+    for i, m, k in mates(n_col, mid, col):
+        push(mine, mine, s_mate.at[i], r_mate.at[i], (outer * 4 + m * 2 + core, k))
+    lax.fori_loop(split, ncols, columns, 0)
+    for i, m, k in mates(n_col, mid, col):
+        await_bytes(mine, s_mate.at[i])
+        await_bytes(mine, r_mate.at[i])
+    half = biaso_ref.at[:, :, core]
+    push(half, half, s_core, r_core, (outer * 4 + mid * 2 + 1 - core, col))
+    await_bytes(half, s_core)
+    await_bytes(half, r_core)
+    for k, ref in ((0, xo_ref), (1, coto_ref)):
+        def arrived(c, carry):
+            await_bytes(ref.at[c, pl.ds(0, n_row - 1)], r_aa.at[k, c])
+            return carry
+
+        lax.fori_loop(0, ncols, arrived, 0)
+        await_bytes(x_ref.at[pl.ds(0, n_row - 1)], s_aa.at[k])
+
+
+def gather(x_tiles, cot_tiles, bias_tile):
+    n_row, ncols, tile_rows, channels = x_tiles.shape
+    n_col = lax.axis_size("col")
+    n_out, n_mates = n_row // 4, 2 * n_col - 1
+    cols = jax.ShapeDtypeStruct((ncols, n_row, tile_rows, channels), BF16)
+    vmem = pl.BlockSpec(memory_space=VM)
+    return pl.pallas_call(
+        gather_kernel,
+        in_specs=[vmem] * 3,
+        out_specs=[vmem] * 3,
+        out_shape=[cols, cols, jax.ShapeDtypeStruct((n_out, 2, 2, n_col) + bias_tile.shape, F32)],
+        scratch_shapes=[
+            DMA((2,)), DMA((2, ncols)), DMA((n_out - 1,)), DMA((n_out - 1,)),
+            DMA((n_mates,)), DMA((n_mates,)), DMA, DMA, DMA((3,)),
+        ],
+        compiler_params=pltpu.CompilerParams(
+            collective_id=0, has_side_effects=True, vmem_limit_bytes=40 * 1024 * 1024
+        ),
+    )(x_tiles, cot_tiles, bias_tile)
+
+
+def scatter_kernel(
+    att_ref, dn_ref, tot_ref, parts_ref, atto_ref, dno_ref, dbias_ref, sums_ref,
+    rbuf, psend, prbuf, zsend, zrecv, qr, qs, qp, qz, qzs,
+    s_aa, r_aa, s_out, r_out, s_mate, r_mate, s_core, r_core, s_ag, r_ag, s_agc, r_agc, s_loc,
+):
+    row, col, outer, mid, core = place()
+    ncols, n_row = att_ref.shape[:2]
+    n_out, n_col = tot_ref.shape[0], tot_ref.shape[3]
+    other = (outer * 4 + mid * 2 + 1 - core, col)
+    meet_all()
+    core_moves = [(tot_ref.at[:, :, 1 - core], rbuf), (parts_ref.at[1 - core], qr)]
+    for i, (src, dst) in enumerate(core_moves):
+        push(src, dst, s_core.at[i], r_core.at[i], other)
+    local = [
+        pltpu.make_async_copy(att_ref.at[:, row], atto_ref.at[row], s_loc.at[0]),
+        pltpu.make_async_copy(dn_ref.at[:, row], dno_ref.at[row], s_loc.at[1]),
+    ]
+    for copy in local:
+        copy.start()
+
+    def columns(c, carry):
+        def peer(i, carry):
+            r = lax.rem(row + i, n_row)
+            push(att_ref.at[c, r], atto_ref.at[row, c], s_aa.at[0], r_aa.at[0], (r, col))
+            push(dn_ref.at[c, r], dno_ref.at[row, c], s_aa.at[1], r_aa.at[1], (r, col))
+            return carry
+
+        return lax.fori_loop(1, n_row, peer, carry)
+
+    split = ncols // 3
+    lax.fori_loop(0, split, columns, 0)
+    for i, (src, dst) in enumerate(core_moves):
+        await_bytes(dst, s_core.at[i])
+        await_bytes(dst, r_core.at[i])
+    for m in range(2):
+        for k in range(n_col):
+            psend[m, k] = (tot_ref[:, m, core, k] + rbuf[:, m, k]).astype(BF16)
+    qs[...] = parts_ref[core] + qr[...]
+    for i, m, k in mates(n_col, mid, col):
+        push(psend.at[m, k], prbuf.at[i], s_mate.at[0, i], r_mate.at[0, i], (outer * 4 + m * 2 + core, k))
+        push(qs.at[m, k], qp.at[i], s_mate.at[1, i], r_mate.at[1, i], (outer * 4 + m * 2 + core, k))
+    lax.fori_loop(split, 2 * split, columns, 0)
+    for i, m, k in mates(n_col, mid, col):
+        for j, ref in ((0, prbuf.at[i]), (1, qp.at[i])):
+            await_bytes(ref, s_mate.at[j, i])
+            await_bytes(ref, r_mate.at[j, i])
+    own = psend[mid, col].astype(F32)
+    mine = qs[mid, col]
+    for i in range(2 * n_col - 1):
+        own += prbuf[i].astype(F32)
+        mine += qp[i]
+    zsend[...] = own
+    qzs[...] = mine
+    for i in range(1, n_out):
+        o = lax.rem(outer + i, n_out)
+        there = (o * 4 + mid * 2 + core, col)
+        push(zsend.at[o], zrecv.at[i - 1], s_out.at[0, i - 1], r_out.at[0, i - 1], there)
+        push(qzs, qz.at[i - 1], s_out.at[1, i - 1], r_out.at[1, i - 1], there)
+    lax.fori_loop(2 * split, ncols, columns, 0)
+    for i in range(n_out - 1):
+        for j, ref in ((0, zrecv.at[i]), (1, qz.at[i])):
+            await_bytes(ref, s_out.at[j, i])
+            await_bytes(ref, r_out.at[j, i])
+    total, sums = zsend[outer], qzs[...]
+    for i in range(n_out - 1):
+        total += zrecv[i]
+        sums += qz[i]
+    dbias_ref[...] = total
+    sums_ref[core, mid, col] = sums
+    slab = sums_ref.at[core, mid, col]
+    for i, m, k in mates(n_col, mid, col):
+        push(slab, slab, s_ag.at[i], r_ag.at[i], (outer * 4 + m * 2 + core, k))
+    for i in range(2 * n_col - 1):
+        await_bytes(slab, s_ag.at[i])
+        await_bytes(slab, r_ag.at[i])
+    half = sums_ref.at[core]
+    push(half, half, s_agc, r_agc, other)
+    await_bytes(half, s_agc)
+    await_bytes(half, r_agc)
+    for copy in local:
+        copy.wait()
+    for k, ref in ((0, atto_ref), (1, dno_ref)):
+        await_bytes(ref.at[pl.ds(0, n_row - 1)], s_aa.at[k])
+        await_bytes(ref.at[pl.ds(0, n_row - 1)], r_aa.at[k])
+
+
+def scatter(att_cols, dn_cols, total, parts):
+    ncols, n_row, tile_rows, channels = att_cols.shape
+    n_out, _, _, n_col = total.shape[:4]
+    tile = total.shape[4:]
+    n_mates, slab = 2 * n_col - 1, parts.shape[3:]
+    tiles = jax.ShapeDtypeStruct((n_row, ncols, tile_rows, channels), BF16)
+    vmem = pl.BlockSpec(memory_space=VM)
+    return pl.pallas_call(
+        scatter_kernel,
+        in_specs=[vmem] * 4,
+        out_specs=[vmem] * 4,
+        out_shape=[
+            tiles, tiles, jax.ShapeDtypeStruct(tile, F32), jax.ShapeDtypeStruct(parts.shape, F32)
+        ],
+        scratch_shapes=[
+            VM((n_out, 2, n_col) + tile, F32),
+            VM((2, n_col, n_out) + tile, BF16),
+            VM((n_mates, n_out) + tile, BF16),
+            VM((n_out,) + tile, F32),
+            VM((n_out - 1,) + tile, F32),
+            VM((2, n_col) + slab, F32),
+            VM((2, n_col) + slab, F32),
+            VM((n_mates,) + slab, F32),
+            VM((n_out - 1,) + slab, F32),
+            VM(slab, F32),
+            DMA((2,)), DMA((2,)), DMA((2, n_out - 1)), DMA((2, n_out - 1)),
+            DMA((2, n_mates)), DMA((2, n_mates)), DMA((2,)), DMA((2,)),
+            DMA((n_mates,)), DMA((n_mates,)), DMA, DMA, DMA((2,)),
+        ],
+        compiler_params=pltpu.CompilerParams(
+            collective_id=1, has_side_effects=True, vmem_limit_bytes=48 * 1024 * 1024
+        ),
+    )(att_cols, dn_cols, total, parts)
+
+
+def share_kernel(mine_ref, sum_ref, got, send, recv):
+    row, col = lax.axis_index("row"), lax.axis_index("col")
+    n_row, n_col = lax.axis_size("row"), lax.axis_size("col")
+    n_all = n_row * n_col
+    meet_all()
+
+    def one(i, carry):
+        there = (lax.rem(row + i // n_col, n_row), lax.rem(col + lax.rem(i, n_col), n_col))
+        push(mine_ref, got.at[i - 1], send, recv, there)
+        return carry
+
+    lax.fori_loop(1, n_all, one, 0)
+    await_bytes(got, send)
+    await_bytes(got, recv)
+    sum_ref[...] = mine_ref[...] + jnp.sum(got[...], axis=0)
+
+
+def share(mine):
+    n_all = lax.axis_size("row") * lax.axis_size("col")
+    vmem = pl.BlockSpec(memory_space=VM)
+    return pl.pallas_call(
+        share_kernel,
+        in_specs=[vmem],
+        out_specs=vmem,
+        out_shape=jax.ShapeDtypeStruct(mine.shape, F32),
+        scratch_shapes=[VM((n_all - 1,) + mine.shape, F32), DMA, DMA],
+        compiler_params=pltpu.CompilerParams(collective_id=2, has_side_effects=True),
+    )(mine)
 
 
 def shards(pair, gain, projections, bias_weight, valid_len, out_cotangent):
@@ -153,44 +420,39 @@
     centered_scaled = (pair_float - average_value) * inverse_deviation
     normalized_pair = (centered_scaled * gain).astype(BF16)
     bias_tile = jnp.einsum("abc,ch->hab", normalized_pair, bias_weight, preferred_element_type=F32)
-    gathered = lax.all_gather(bias_tile[None], ("row", "col"), axis=0, tiled=True)
-    gathered = gathered.reshape(n_row, n_col, heads, tile_rows, tile_cols)
 
     def to_columns(tile):
-        moved = jnp.swapaxes(tile, 0, 1).reshape(n_row, ncols, tile_rows, channels)
-        return lax.all_to_all(moved, "row", split_axis=0, concat_axis=0, tiled=True)
+        return jnp.swapaxes(tile, 0, 1).reshape(n_row, ncols, tile_rows, channels)
 
     def to_tile(columns):
-        moved = lax.all_to_all(columns, "row", split_axis=0, concat_axis=0, tiled=True)
-        return jnp.swapaxes(moved.reshape(tile_cols, tile_rows, channels), 0, 1)
-
-    x_cols, cot_cols = to_columns(normalized_pair), to_columns(out_cotangent)
+        return jnp.swapaxes(columns.reshape(tile_cols, tile_rows, channels), 0, 1)
+
+    x_cols, cot_cols, bias = gather(to_columns(normalized_pair), to_columns(out_cotangent), bias_tile)
     w_in = jnp.swapaxes(projections[:4], 0, 1).reshape(channels, 4 * channels)
     att_cols, dn_cols, total, parts = attention(
-        valid_len, x_cols, cot_cols, w_in, projections[4], gathered
-    )
-    everyone = ("row", "col")
-    n_all = n_row * n_col
-
-    def swap(blocks):
-        return lax.all_to_all(blocks, everyone, split_axis=0, concat_axis=0, tiled=True)
-
-    shares = swap(total.reshape(n_all, heads, tile_rows, tile_cols))
-    d_bias = jnp.sum(shares.astype(F32), axis=0).astype(BF16)
+        valid_len, x_cols, cot_cols, w_in, projections[4],
+        bias.reshape(n_row, n_col, heads, tile_rows, tile_cols),
+    )
     parts = jnp.swapaxes(parts.reshape(channels, 5, channels), 0, 1)
-    slab = 5 * channels // n_all
-    owned = jnp.sum(swap(parts.reshape(n_all, slab, channels)), axis=0)
-    attended = to_tile(att_cols)
+    att_tile, dn_tile, total, sums = scatter(
+        att_cols, dn_cols,
+        total.reshape(n_row // 4, 2, 2, n_col, heads, tile_rows, tile_cols),
+        parts.reshape(2, 2, n_col, 5 * channels // (4 * n_col), channels),
+    )
+    projection_grad = sums.reshape(5, channels, channels)
+    d_bias = total.astype(BF16)
+    attended = to_tile(att_tile)
     bias_term = jnp.einsum("hab,ch->abc", d_bias, bias_weight, preferred_element_type=F32)
     bias_weight_part = jnp.einsum(
         "hab,abc->hc", d_bias, normalized_pair, preferred_element_type=F32
     )
-    normalized_gradient = to_tile(dn_cols).astype(F32) + bias_term
+    normalized_gradient = to_tile(dn_tile).astype(F32) + bias_term
     gain_partial_sum = jnp.sum(normalized_gradient * centered_scaled, axis=(0, 1))
-    mine = jnp.concatenate([owned, bias_weight_part, gain_partial_sum[None]], axis=0)
-    spread = swap(jnp.broadcast_to(mine[None], (n_all,) + mine.shape))
-    projection_grad = spread[:, :slab].reshape(5, channels, channels)
-    small = jnp.sum(spread[:, slab:], axis=0)
+    small = share(
+        jnp.concatenate(
+            [bias_weight_part, gain_partial_sum[None], jnp.zeros((7 - heads % 8, channels), F32)], axis=0
+        )
+    )
     bias_weight_grad, gain_gradient = small[:heads].T, small[heads]
     scaled_output = normalized_gradient * gain
     pair_gradient = inverse_deviation * (

time: 303 us -> 233 us (0.77)
  Pallas kernels: 46.4 us -> 193 us
  blocking collectives: 93.4 us -> 0 us
  waiting for transfers between devices: 75.2 us -> 0 us
  starting transfers between devices: 28.8 us -> 0 us
  between operations: 15 us -> 1.49 us
  other arithmetic: 16.3 us -> 13.2 us
    pallas_call x0 -> x3, Pallas kernels: none -> 146 us  [the longest x1 69.5 us: scatter(): pl.pallas_call(scatter_kernel, in_specs=[vmem] * 4, out_specs=[vmem] * 4,...]
    all_to_all x3 -> x0, blocking collectives: 93.4 us -> none  [the longest x2 60.6 us: swap(): lax.all_to_all(blocks, everyone, split_axis=0, concat_axis=0, tiled=True)]
    all_to_all x4 -> x0, waiting for transfers between devices: 75.2 us -> none  [the longest x2 55.4 us: to_columns(): return lax.all_to_all(moved, 'row', split_axis=0, concat_axis=0, tiled=True)]
    all_to_all x4 -> x0, starting transfers between devices: 28.7 us -> none  [the longest x2 16.4 us: to_columns(): return lax.all_to_all(moved, 'row', split_axis=0, concat_axis=0, tiled=True)]
    unnamed x42 -> x21, local copies, waits for them, and re-layouts: 1.74 us -> 6.97 us
  transfers between devices with their start and end apart: 5 -> 0, of which waited for: 4 -> 0; matrix products, arithmetic and copies ran while one was open for 9% -> 0% of each run, Pallas kernels for 0% -> 0%
where the time goes in v1:
time: 233 us; the launch traced here: 232 us
  Pallas kernels  193 us (83%)
  local copies, waits for them, and re-layouts  14.9 us (6%)
  other arithmetic  13.2 us (6%)
  matrix products  9.19 us (4%)
    pallas_call x1, Pallas kernels, scatter(): pl.pallas_call(scatter_kernel, in_specs=[vmem] * 4, out_specs=[vmem] * 4,...  69.5 us
    pallas_call x1, Pallas kernels, gather(): pl.pallas_call(gather_kernel, in_specs=[vmem] * 3, out_specs=[vmem] * 3,...  66.9 us
    pallas_call x1, Pallas kernels, attention(): pl.pallas_call(functools.partial(attention_kernel, heads), grid=(ncols,),...  46.9 us
    pallas_call x1, Pallas kernels, share(): pl.pallas_call(share_kernel, in_specs=[vmem], out_specs=vmem, out_shape=j...  10 us
    unnamed x21, local copies, waits for them, and re-layouts  6.97 us
    mul x1, other arithmetic, shards(): inverse_deviation * (scaled_output - jnp.mean(scaled_output, axis=-1, kee...  6.13 us
    dot_general x1, matrix products, shards(): jnp.einsum('hab,ch->abc', d_bias, bias_weight, preferred_element_type=F32)  5.41 us

profile of v1, /device:TPU:0, one launch (start us, length us, event | category | flops | bytes accessed | tf_op | source)
XLA Modules:
  0.0 232.0 jit_solution(10776837950587626394)
XLA Ops:
  0.6 0.0 copy-start
  0.6 0.0 copy-start.6
  0.7 0.0 copy-start.9
  0.7 1.9 convert_reduce_fusion
  2.5 2.8 %fusion.11 = f32[24,192]{1,0:T(8,128)S(1)} fusion(bf16[24,192,128]{2,1,0:T(8,128)(2,1)} %param.6, f32[24,192]{1,0:T(8,128)S(1)} %broadcast_multiply_fusion.2), kind=kLoop, calls=%fused_computation.13 | loop fusion | flops 2354688 | bytes 1216512 | tf_op jit(solution)/shard_map/reduce_sum | solution.py:418
  5.4 0.0 copy-done.6
  5.4 0.0 copy-done.9
  5.4 1.5 fusion.15
  6.8 0.0 copy-start.7
  6.8 0.8 copy.20
  7.6 0.0 copy-done
  7.6 2.0 fusion.13
  9.6 0.0 copy-done.7
  9.7 0.0 copy-start.8
  9.7 0.8 copy.21
  10.4 66.9 %shard_map.101 = (bf16[12,16,24,128]{3,2,1,0:T(8,128)(2,1)S(1)}, bf16[12,16,24,128]{3,2,1,0:T(8,128)(2,1)S(1)}, f32[4,2,2,2,4,24,192]{6,5,4,3,2,1,0:T(8,128)S(1)}) custom-call(bf16[16,12,24,128]{3,2,1,0:T(8,128)(2,1)S(1)} %bitcast.46, bf16[16,12,24,128]{3,2,1,0:T(8,128)(2,1)S(1)} %bitcast.47, f32[4,24,192]{2,1,0:T(8,128)S(1)} %bitcast.51), custom_call_target="tpu_custom_call" | custom-call | tf_op jit(solution)/shard_map/pallas_call | solution.py:244
  77.4 0.0 copy-start.1
  77.4 1.7 copy-done.1
  79.0 0.0 copy-start.4
  79.0 1.0 copy-done.4
  80.0 0.0 copy-start.5
  80.0 1.0 copy-done.5
  81.1 0.0 copy-done.8
  81.1 0.7 copy_bitcast_fusion.1.w_in_ref
  81.7 0.6 slice_bitcast_fusion.1.w_out_ref
  83.0 46.9 %shard_map.102 = (bf16[12,16,24,128]{3,2,1,0:T(8,128)(2,1)}, bf16[12,16,24,128]{3,2,1,0:T(8,128)(2,1)}, f32[16,2,4,24,192]{4,3,2,1,0:T(8,128)}, f32[128,640]{1,0:T(8,128)}) custom-call(s32[1]{0:T(128)S(6)} %copy.44.valid_ref, bf16[12,16,24,128]{3,2,1,0:T(8,128)(2,1)} %copy-done.4, bf16[12,16,24,128]{3,2,1,0:T(8,128)(2,1)} %copy-done.5, ...), custom_call_target="tpu_custom_call" | custom-call | tf_op jit(solution)/shard_map/pallas_call | solution.py:115
  129.9 1.1 copy.24
  131.0 0.2 copy.25
  131.2 0.0 copy-start.2
  131.2 1.3 copy-done.2
  132.5 0.0 copy-start.3
  132.5 1.3 copy-done.3
  133.7 69.5 %shard_map.103 = (bf16[16,12,24,128]{3,2,1,0:T(8,128)(2,1)S(1)}, bf16[16,12,24,128]{3,2,1,0:T(8,128)(2,1)S(1)}, f32[4,24,192]{2,1,0:T(8,128)S(1)}, f32[2,2,2,80,128]{4,3,2,1,0:T(8,128)S(1)}) custom-call(bf16[12,16,24,128]{3,2,1,0:T(8,128)(2,1)S(1)} %copy-done.2, bf16[12,16,24,128]{3,2,1,0:T(8,128)(2,1)S(1)} %copy-done.3, ...), custom_call_target="tpu_custom_call" | custom-call | tf_op jit(solution)/shard_map/pallas_call | solution.py:352
  203.2 0.2 bitcast_convert_fusion
  203.5 5.4 %fusion.10 = (f32[128]{0:T(128)S(1)}, f32[24,192]{1,0:T(8,128)S(1)}, f32[24,192]{1,0:T(8,128)S(1)}, f32[24,192,128]{2,1,0:T(8,128)}) fusion(bf16[24,192,128]{2,1,0:T(8,128)(2,1)S(1)} %copy-done.6, f32[24,192]{1,0:T(8,128)S(1)} %add_rsqrt_fusion, f32[24,192]{1,0:T(8,128)S(1)} %broadcast_multiply_fusion.2, f32[128]{0:T(128)S(1)} %copy-done.9, ...), kind=kOutput, calls=%fused_computation.12 | convolution fusion | flops 10607488 | bytes 6010880 | tf_op jit(solution)/shard_map/hab,ch->abc/dot_general | solution.py:445
  208.9 1.8 convolution_bitcast_fusion
  210.7 0.1 pad.2.clone
  210.8 0.7 maximum_maximum_fusion.mine_ref
  211.5 10.0 %shard_map.104 = f32[8,128]{1,0:T(8,128)} custom-call(f32[8,128]{1,0:T(8,128)} %maximum_maximum_fusion.mine_ref), custom_call_target="tpu_custom_call" | custom-call | tf_op jit(solution)/shard_map/pallas_call | solution.py:400
  221.5 1.2 slice_bitcast_fusion.2
  222.7 1.2 slice_bitcast_fusion.3
  223.9 6.1 %fusion.9 = f32[24,192,128]{2,1,0:T(8,128)} fusion(bf16[24,192,128]{2,1,0:T(8,128)(2,1)S(1)} %copy-done.6, f32[24,192,128]{2,1,0:T(8,128)} %get-tuple-element.30, f32[24,192]{1,0:T(8,128)S(1)} %get-tuple-element.31, f32[24,192]{1,0:T(8,128)S(1)} %get-tuple-element.32, f32[128]{0:T(128)S(1)} %copy-done.9, f32[24,192]{1,0:T(8,128)S(1)} %add_rsqrt_fusion, ...), kind=kLoop, calls=%fused_computation.11 | loop fusion | flops 4718592 | bytes 5972480 | tf_op jit(solution)/shard_map/mul | solution.py:458
  230.0 1.3 copy.41
  231.3 0.7 copy.45
  (6 shorter events, 0.1 us)
Async XLA Ops:
  0.6 7.0 %copy-start = (bf16[128,4]{0,1:T(4,128)(2,1)S(1)}, bf16[128,4]{0,1:T(4,128)(2,1)}, u32[]{:S(2)}) copy-start(bf16[128,4]{0,1:T(4,128)(2,1)} %param.9) | copy-start | bytes 3076
  0.6 4.7 %copy-start.6 = (bf16[24,192,128]{2,1,0:T(8,128)(2,1)S(1)}, bf16[24,192,128]{2,1,0:T(8,128)(2,1)}, u32[]{:S(2)}) copy-start(bf16[24,192,128]{2,1,0:T(8,128)(2,1)} %param.6) | copy-start | bytes 3538948
  0.7 4.7 %copy-start.9 = (f32[128]{0:T(128)S(1)}, f32[128]{0:T(128)}, u32[]{:S(2)}) copy-start(f32[128]{0:T(128)} %param.7) | copy-start | bytes 1540
  6.8 2.8 %copy-start.7 = (bf16[24,192,128]{2,1,0:T(8,128)(2,1)S(1)}, bf16[24,192,128]{2,1,0:T(8,128)(2,1)}, u32[]{:S(2)}) copy-start(bf16[24,192,128]{2,1,0:T(8,128)(2,1)} %param.11) | copy-start | bytes 3538948
  9.7 71.4 %copy-start.8 = (bf16[5,128,128]{2,1,0:T(8,128)(2,1)S(1)}, bf16[5,128,128]{2,1,0:T(8,128)(2,1)}, u32[]{:S(2)}) copy-start(bf16[5,128,128]{2,1,0:T(8,128)(2,1)} %param.8) | copy-start | bytes 491524
  77.4 1.7 copy-start.1
  79.0 1.0 copy-start.4
  80.0 1.0 copy-start.5
  131.2 1.3 copy-start.2
  132.5 1.3 copy-start.3

commit v2 on v0

v2 whole, which is shorter than its diff:
```python
import functools

import jax
import jax.numpy as jnp
from jax import lax
from jax.experimental import pallas as pl
from jax.experimental.pallas import tpu as pltpu
from jax.sharding import PartitionSpec as P

EPS = 1e-05
F32 = jnp.float32
BF16 = jnp.bfloat16


def mm(left, right):
    return lax.dot_general(left, right, (((1,), (0,)), ((), ())), preferred_element_type=F32)


def mm_nt(left, right):
    return lax.dot_general(left, right, (((1,), (1,)), ((), ())), preferred_element_type=F32)


MESH = pl.DeviceIdType.MESH
VM = pltpu.VMEM
DMA = pltpu.SemaphoreType.DMA


def place():
    row, col = lax.axis_index("row"), lax.axis_index("col")
    return row, col, row // 4, lax.rem(row // 2, 2), lax.rem(row, 2)


def meet_all():
    row, col = lax.axis_index("row"), lax.axis_index("col")
    n_row, n_col = lax.axis_size("row"), lax.axis_size("col")
    barrier = pltpu.get_barrier_semaphore()

    def greet(i, carry):
        there = (lax.rem(row + i // n_col, n_row), lax.rem(col + lax.rem(i, n_col), n_col))
        pl.semaphore_signal(barrier, inc=1, device_id=there, device_id_type=MESH)
        return carry

    lax.fori_loop(1, n_row * n_col, greet, 0)
    pl.semaphore_wait(barrier, n_row * n_col - 1)


def push(src, dst, send, recv, where):
    pltpu.make_async_remote_copy(
        src_ref=src, dst_ref=dst, send_sem=send, recv_sem=recv,
        device_id=where, device_id_type=MESH,
    ).start()


def await_bytes(ref, sem):
    pltpu.make_async_copy(ref, ref, sem).wait()


def mates(n_col, mid, col):
    for i in range(1, 2 * n_col):
        yield i - 1, lax.rem(mid + i // n_col, 2), lax.rem(col + i % n_col, n_col)


def attend(heads, valid_ref, x_ref, cot_ref, w_in_ref, w_out_ref, bias_s, dbias_s, parts_ref, att_ref, dn_ref):
    n_row, tile_rows, channels = x_ref.shape
    rows = n_row * tile_rows
    width = channels // heads
    scale = width ** (-0.5)
    keep_lanes = lax.broadcasted_iota(jnp.int32, (rows, 1), 0) < valid_ref[0]
    x = x_ref[...].astype(F32).reshape(rows, channels).astype(BF16)
    cot = cot_ref[...].astype(F32).reshape(rows, channels).astype(BF16)
    proj = mm(x, w_in_ref[...])
    query = proj[:, :channels].astype(BF16)
    key_f = jnp.where(keep_lanes, proj[:, channels : 2 * channels], 0.0)
    key = key_f.astype(BF16)
    value_f = proj[:, 2 * channels : 3 * channels]
    value = value_f.astype(BF16)
    gate = jax.nn.sigmoid(proj[:, 3 * channels :])
    d_gated = mm_nt(cot, w_out_ref[...])
    d_context_f = d_gated * gate
    d_context = d_context_f.astype(BF16)
    key_t = jnp.transpose(key_f).astype(BF16)
    value_t = jnp.transpose(value_f).astype(BF16)
    lane_head = lax.broadcasted_iota(jnp.int32, (rows, channels), 1) // width
    ctx_parts, dq_parts = [], []
    dk = jnp.zeros((rows, channels), F32)
    dv = jnp.zeros((rows, channels), F32)
    for h in range(heads):
        mine = lane_head == h
        q_h = jnp.where(mine, query, jnp.zeros_like(query))
        dc_h = jnp.where(mine, d_context, jnp.zeros_like(d_context))
        s = mm_nt(key, q_h) * scale + bias_s[h]
        e = jnp.exp(s - jnp.max(s, axis=0, keepdims=True))
        p = e * (1.0 / jnp.sum(e, axis=0, keepdims=True))
        d_p = mm_nt(value, dc_h)
        delta = jnp.sum(p * d_p, axis=0, keepdims=True)
        ds = p * (d_p - delta)
        dbias_s[h] += ds
        p_b = p.astype(BF16)
        ds_b = ds.astype(BF16)
        ctx_parts.append(mm(value_t[h * width : (h + 1) * width], p_b))
        dq_parts.append(mm(key_t[h * width : (h + 1) * width], ds_b))
        dv += mm(p_b, dc_h)
        dk += mm(ds_b, q_h)
    context = jnp.transpose(jnp.concatenate(ctx_parts, axis=0)).astype(BF16).astype(F32)
    dq = (jnp.transpose(jnp.concatenate(dq_parts, axis=0)) * scale).astype(BF16)
    dk = (dk * scale).astype(BF16)
    dv = dv.astype(BF16)
    gated_f = gate * context
    gated = gated_f.astype(BF16)
    att = mm(gated, w_out_ref[...])
    att_ref[...] = att.reshape(n_row, tile_rows, channels).astype(att_ref.dtype)
    d_gate = (d_gated * context * gate * (1.0 - gate)).astype(BF16)
    grads = jnp.concatenate([dq, dk, dv, d_gate], axis=1)
    dn = mm_nt(grads, w_in_ref[...])
    dn_ref[...] = dn.reshape(n_row, tile_rows, channels).astype(dn_ref.dtype)
    x_t = jnp.transpose(x.astype(F32)).astype(BF16)
    parts_ref[:, : 4 * channels] += mm(x_t, grads)
    gated_t = jnp.transpose(gated.astype(F32)).astype(BF16)
    parts_ref[:, 4 * channels :] += mm(gated_t, cot)


def layer_kernel(
    heads, valid_ref, x_ref, cot_ref, bias_ref, w_in_ref, w_out_ref,
    atto_ref, dno_ref, dbias_ref, sums_ref,
    xc, cc, ball, bias_s, dbias_s, parts_s, att_s, dn_s,
    rbuf, psend, prbuf, zsend, zrecv, parts_c, qr, qs, qp, qz, qzs,
    s_fw, r_fw, s_bw, r_bw, s_bo, r_bo, s_bm, r_bm, s_bc, r_bc,
    s_out, r_out, s_mate, r_mate, s_core, r_core, s_ag, r_ag, s_agc, r_agc, s_loc,
):
    row, col, outer, mid, core = place()
    n_row, ncols, tile_rows, channels = x_ref.shape
    n_out, n_col = ball.shape[0], ball.shape[3]
    tile_cols = bias_ref.shape[2]
    rows = n_row * tile_rows
    other = (outer * 4 + mid * 2 + 1 - core, col)
    meet_all()
    for i in range(1, n_out):
        there = lax.rem(outer + i, n_out) * 4 + mid * 2 + core
        push(bias_ref, ball.at[outer, mid, core, col], s_bo.at[i - 1], r_bo.at[i - 1], (there, col))
    local = [
        pltpu.make_async_copy(bias_ref, ball.at[outer, mid, core, col], s_loc.at[0]),
        pltpu.make_async_copy(x_ref.at[row], xc.at[:, row], s_loc.at[1]),
        pltpu.make_async_copy(cot_ref.at[row], cc.at[:, row], s_loc.at[2]),
    ]
    for copy in local:
        copy.start()

    def send_out(c, carry):
        def peer(i, carry):
            r = lax.rem(row + i, n_row)
            push(x_ref.at[r, c], xc.at[c, row], s_fw.at[0], r_fw.at[0, c], (r, col))
            push(cot_ref.at[r, c], cc.at[c, row], s_fw.at[1], r_fw.at[1, c], (r, col))
            return carry

        return lax.fori_loop(1, n_row, peer, carry)

    def send_back(c, carry):
        def peer(i, carry):
            r = lax.rem(row + i, n_row)
            push(att_s.at[c, r], atto_ref.at[row, c], s_bw.at[0], r_bw.at[0], (r, col))
            push(dn_s.at[c, r], dno_ref.at[row, c], s_bw.at[1], r_bw.at[1], (r, col))
            return carry

        return lax.fori_loop(1, n_row, peer, carry)

    early = (ncols + 3) // 4
    lax.fori_loop(0, early, send_out, 0)
    dbias_s[...] = jnp.zeros_like(dbias_s)
    parts_s[...] = jnp.zeros_like(parts_s)
    for copy in local:
        copy.wait()
    for i in range(1, n_out):
        await_bytes(bias_ref, s_bo.at[i - 1])
        await_bytes(bias_ref, r_bo.at[i - 1])
    mine = ball.at[:, mid, core, col]
    for i, m, k in mates(n_col, mid, col):
        push(mine, mine, s_bm.at[i], r_bm.at[i], (outer * 4 + m * 2 + core, k))
    lax.fori_loop(early, ncols, send_out, 0)
    for i in range(2 * n_col - 1):
        await_bytes(mine, s_bm.at[i])
        await_bytes(mine, r_bm.at[i])
    half = ball.at[:, :, core]
    push(half, half, s_bc, r_bc, other)
    await_bytes(half, s_bc)
    await_bytes(half, r_bc)
    keep_lanes = lax.broadcasted_iota(jnp.int32, (rows, 1), 0) < valid_ref[0]
    for h in range(heads):
        for k in range(n_col):
            block = ball[:, :, :, k, h].reshape(rows, tile_cols)
            bias_s[h, :, k * tile_cols : (k + 1) * tile_cols] = jnp.where(keep_lanes, block, -1000000000.0)

    held = ncols * 5 // 12

    def column(c, carry):
        await_bytes(xc.at[c, pl.ds(0, n_row - 1)], r_fw.at[0, c])
        await_bytes(cc.at[c, pl.ds(0, n_row - 1)], r_fw.at[1, c])

        @pl.when((c > 0) & (c <= ncols - held))
        def _():
            send_back(c - 1, 0)

        attend(
            heads, valid_ref, xc.at[c], cc.at[c], w_in_ref, w_out_ref,
            bias_s, dbias_s, parts_s, att_s.at[c], dn_s.at[c],
        )
        return carry

    lax.fori_loop(0, ncols, column, 0)

    for h in range(heads):
        for k in range(n_col):
            block = dbias_s[h, :, k * tile_cols : (k + 1) * tile_cols]
            ball[:, :, :, k, h] = block.reshape(n_out, 2, 2, tile_rows, tile_cols)
    slab = parts_c.shape[3]
    for j in range(5 * channels // slab):
        lo = j * slab
        if channels % slab == 0:
            piece = parts_s[lo % channels : lo % channels + slab, lo // channels * channels : (lo // channels + 1) * channels]
        else:
            first = min(slab, channels - lo % channels)
            m = lo // channels
            piece = parts_s[lo % channels : lo % channels + first, m * channels : (m + 1) * channels]
            if first < slab:
                piece = jnp.concatenate([piece, parts_s[: slab - first, (m + 1) * channels : (m + 2) * channels]], axis=0)
        parts_c[j // (2 * n_col), j // n_col % 2, j % n_col] = piece
    core_moves = [(ball.at[:, :, 1 - core], rbuf), (parts_c.at[1 - core], qr)]
    for i, (src, dst) in enumerate(core_moves):
        push(src, dst, s_core.at[i], r_core.at[i], other)
    local = [
        pltpu.make_async_copy(att_s.at[:, row], atto_ref.at[row], s_loc.at[0]),
        pltpu.make_async_copy(dn_s.at[:, row], dno_ref.at[row], s_loc.at[1]),
    ]
    for copy in local:
        copy.start()
    for i, (src, dst) in enumerate(core_moves):
        await_bytes(dst, s_core.at[i])
        await_bytes(dst, r_core.at[i])
    for m in range(2):
        for k in range(n_col):
            psend[m, k] = (ball[:, m, core, k] + rbuf[:, m, k]).astype(BF16)
    qs[...] = parts_c[core] + qr[...]
    for i, m, k in mates(n_col, mid, col):
        push(psend.at[m, k], prbuf.at[i], s_mate.at[0, i], r_mate.at[0, i], (outer * 4 + m * 2 + core, k))
        push(qs.at[m, k], qp.at[i], s_mate.at[1, i], r_mate.at[1, i], (outer * 4 + m * 2 + core, k))
    for i in range(2 * n_col - 1):
        for j, ref in ((0, prbuf.at[i]), (1, qp.at[i])):
            await_bytes(ref, s_mate.at[j, i])
            await_bytes(ref, r_mate.at[j, i])
    own = psend[mid, col].astype(F32)
    mine = qs[mid, col]
    for i in range(2 * n_col - 1):
        own += prbuf[i].astype(F32)
        mine += qp[i]
    zsend[...] = own
    qzs[...] = mine
    for i in range(1, n_out):
        o = lax.rem(outer + i, n_out)
        there = (o * 4 + mid * 2 + core, col)
        push(zsend.at[o], zrecv.at[i - 1], s_out.at[0, i - 1], r_out.at[0, i - 1], there)
        push(qzs, qz.at[i - 1], s_out.at[1, i - 1], r_out.at[1, i - 1], there)
    lax.fori_loop(ncols - held, ncols, send_back, 0)
    for i in range(n_out - 1):
        for j, ref in ((0, zrecv.at[i]), (1, qz.at[i])):
            await_bytes(ref, s_out.at[j, i])
            await_bytes(ref, r_out.at[j, i])
    total, sums = zsend[outer], qzs[...]
    for i in range(n_out - 1):
        total += zrecv[i]
        sums += qz[i]
    dbias_ref[...] = total
    sums_ref[core, mid, col] = sums
    slab = sums_ref.at[core, mid, col]
    for i, m, k in mates(n_col, mid, col):
        push(slab, slab, s_ag.at[i], r_ag.at[i], (outer * 4 + m * 2 + core, k))
    for i in range(2 * n_col - 1):
        await_bytes(slab, s_ag.at[i])
        await_bytes(slab, r_ag.at[i])
    half = sums_ref.at[core]
    push(half, half, s_agc, r_agc, other)
    await_bytes(half, s_agc)
    await_bytes(half, r_agc)
    for copy in local:
        copy.wait()
    for k, ref in ((0, atto_ref), (1, dno_ref)):
        await_bytes(x_ref.at[pl.ds(0, n_row - 1)], s_fw.at[k])
        await_bytes(ref.at[pl.ds(0, n_row - 1)], s_bw.at[k])
        await_bytes(ref.at[pl.ds(0, n_row - 1)], r_bw.at[k])


def layer(valid_len, x_tiles, cot_tiles, bias_tile, w_in, w_out):
    n_row, ncols, tile_rows, channels = x_tiles.shape
    n_col = lax.axis_size("col")
    heads, _, tile_cols = tile = bias_tile.shape
    n_out, n_mates, rows = n_row // 4, 2 * n_col - 1, n_row * tile_rows
    slab = (5 * channels // (4 * n_col), channels)
    tiles = jax.ShapeDtypeStruct(x_tiles.shape, BF16)
    vmem = pl.BlockSpec(memory_space=VM)
    cols = VM((ncols, n_row, tile_rows, channels), BF16)
    return pl.pallas_call(
        functools.partial(layer_kernel, heads),
        in_specs=[pl.BlockSpec(memory_space=pltpu.SMEM)] + [vmem] * 5,
        out_specs=[vmem] * 4,
        out_shape=[
            tiles, tiles, jax.ShapeDtypeStruct(tile, F32),
            jax.ShapeDtypeStruct((2, 2, n_col) + slab, F32),
        ],
        scratch_shapes=[
            cols, cols,
            VM((n_out, 2, 2, n_col) + tile, F32),
            VM((heads, rows, rows), F32),
            VM((heads, rows, rows), F32),
            VM((channels, 5 * channels), F32),
            cols, cols,
            VM((n_out, 2, n_col) + tile, F32),
            VM((2, n_col, n_out) + tile, BF16),
            VM((n_mates, n_out) + tile, BF16),
            VM((n_out,) + tile, F32),
            VM((n_out - 1,) + tile, F32),
            VM((2, 2, n_col) + slab, F32),
            VM((2, n_col) + slab, F32),
            VM((2, n_col) + slab, F32),
            VM((n_mates,) + slab, F32),
            VM((n_out - 1,) + slab, F32),
            VM(slab, F32),
            DMA((2,)), DMA((2, ncols)), DMA((2,)), DMA((2,)),
            DMA((n_out - 1,)), DMA((n_out - 1,)), DMA((n_mates,)), DMA((n_mates,)), DMA, DMA,
            DMA((2, n_out - 1)), DMA((2, n_out - 1)),
            DMA((2, n_mates)), DMA((2, n_mates)), DMA((2,)), DMA((2,)),
            DMA((n_mates,)), DMA((n_mates,)), DMA, DMA, DMA((3,)),
        ],
        compiler_params=pltpu.CompilerParams(
            collective_id=0, has_side_effects=True, vmem_limit_bytes=60 * 1024 * 1024
        ),
    )(valid_len, x_tiles, cot_tiles, bias_tile, w_in, w_out)


def share_kernel(mine_ref, sum_ref, got, send, recv):
    row, col = lax.axis_index("row"), lax.axis_index("col")
    n_row, n_col = lax.axis_size("row"), lax.axis_size("col")
    n_all = n_row * n_col
    meet_all()

    def one(i, carry):
        there = (lax.rem(row + i // n_col, n_row), lax.rem(col + lax.rem(i, n_col), n_col))
        push(mine_ref, got.at[i - 1], send, recv, there)
        return carry

    lax.fori_loop(1, n_all, one, 0)
    await_bytes(got, send)
    await_bytes(got, recv)
    sum_ref[...] = mine_ref[...] + jnp.sum(got[...], axis=0)


def share(mine):
    n_all = lax.axis_size("row") * lax.axis_size("col")
    vmem = pl.BlockSpec(memory_space=VM)
    return pl.pallas_call(
        share_kernel,
        in_specs=[vmem],
        out_specs=vmem,
        out_shape=jax.ShapeDtypeStruct(mine.shape, F32),
        scratch_shapes=[VM((n_all - 1,) + mine.shape, F32), DMA, DMA],
        compiler_params=pltpu.CompilerParams(collective_id=1, has_side_effects=True),
    )(mine)


def shards(pair, gain, projections, bias_weight, valid_len, out_cotangent):
    n_row = lax.axis_size("row")
    n_col = lax.axis_size("col")
    tile_rows, tile_cols, channels = pair.shape
    heads = bias_weight.shape[1]
    ncols = tile_cols // n_row
    pair_float = pair.astype(F32)
    average_value = jnp.mean(pair_float, axis=-1, keepdims=True)
    var = jnp.mean((pair_float - average_value) ** 2, axis=-1, keepdims=True)
    inverse_deviation = lax.rsqrt(var + EPS)
    centered_scaled = (pair_float - average_value) * inverse_deviation
    normalized_pair = (centered_scaled * gain).astype(BF16)
    bias_tile = jnp.einsum("abc,ch->hab", normalized_pair, bias_weight, preferred_element_type=F32)

    def to_columns(tile):
        return jnp.swapaxes(tile, 0, 1).reshape(n_row, ncols, tile_rows, channels)

    def to_tile(columns):
        return jnp.swapaxes(columns.reshape(tile_cols, tile_rows, channels), 0, 1)

    w_in = jnp.swapaxes(projections[:4], 0, 1).reshape(channels, 4 * channels)
    att_tile, dn_tile, total, sums = layer(
        valid_len, to_columns(normalized_pair), to_columns(out_cotangent), bias_tile, w_in, projections[4]
    )
    projection_grad = sums.reshape(5, channels, channels)
    d_bias = total.astype(BF16)
    attended = to_tile(att_tile)
    bias_term = jnp.einsum("hab,ch->abc", d_bias, bias_weight, preferred_element_type=F32)
    bias_weight_part = jnp.einsum(
        "hab,abc->hc", d_bias, normalized_pair, preferred_element_type=F32
    )
    normalized_gradient = to_tile(dn_tile).astype(F32) + bias_term
    gain_partial_sum = jnp.sum(normalized_gradient * centered_scaled, axis=(0, 1))
    small = share(
        jnp.concatenate(
            [bias_weight_part, gain_partial_sum[None], jnp.zeros((7 - heads % 8, channels), F32)], axis=0
        )
    )
    bias_weight_grad, gain_gradient = small[:heads].T, small[heads]
    scaled_output = normalized_gradient * gain
    pair_gradient = inverse_deviation * (
        scaled_output
        - jnp.mean(scaled_output, axis=-1, keepdims=True)
        - centered_scaled * jnp.mean(scaled_output * centered_scaled, axis=-1, keepdims=True)
    )
    return (attended, pair_gradient, projection_grad, bias_weight_grad, gain_gradient)


def solution(mesh):
    placed = (P("row", "col", None), P(), P(), P(), P(), P("row", "col", None))
    return jax.shard_map(
        shards,
        mesh=mesh,
        in_specs=placed,
        out_specs=(P("row", "col", None), P("row", "col", None), P(), P(), P()),
        check_vma=False,
    )
```

time: 303 us -> 198 us (0.65)
  Pallas kernels: 46.4 us -> 162 us
  blocking collectives: 93.4 us -> 0 us
  waiting for transfers between devices: 75.2 us -> 0 us
  starting transfers between devices: 28.8 us -> 0 us
  between operations: 15 us -> 1.42 us
  local copies, waits for them, and re-layouts: 17.4 us -> 10.1 us
    pallas_call x1 -> x2, Pallas kernels: 46.4 us -> 162 us  [the longest x1 153 us: layer(): pl.pallas_call(functools.partial(layer_kernel, heads), in_specs=[pl.Block...]
    all_to_all x3 -> x0, blocking collectives: 93.4 us -> none  [the longest x2 60.6 us: swap(): lax.all_to_all(blocks, everyone, split_axis=0, concat_axis=0, tiled=True)]
    all_to_all x4 -> x0, waiting for transfers between devices: 75.2 us -> none  [the longest x2 55.4 us: to_columns(): return lax.all_to_all(moved, 'row', split_axis=0, concat_axis=0, tiled=True)]
    all_to_all x4 -> x0, starting transfers between devices: 28.7 us -> none  [the longest x2 16.4 us: to_columns(): return lax.all_to_all(moved, 'row', split_axis=0, concat_axis=0, tiled=True)]
  transfers between devices with their start and end apart: 5 -> 0, of which waited for: 4 -> 0; matrix products, arithmetic and copies ran while one was open for 9% -> 0% of each run, Pallas kernels for 0% -> 0%
where the time goes in v2:
time: 198 us
  Pallas kernels  162 us (82%)
  other arithmetic  15.8 us (8%)
  local copies, waits for them, and re-layouts  10.1 us (5%)
  matrix products  8.33 us (4%)
    pallas_call x1, Pallas kernels, layer(): pl.pallas_call(functools.partial(layer_kernel, heads), in_specs=[pl.Block...  153 us
    pallas_call x1, Pallas kernels, share(): pl.pallas_call(share_kernel, in_specs=[vmem], out_specs=vmem, out_shape=j...  9.68 us
    mul x1, other arithmetic, shards(): inverse_deviation * (scaled_output - jnp.mean(scaled_output, axis=-1, kee...  5.95 us
    dot_general x1, matrix products, shards(): jnp.einsum('hab,ch->abc', d_bias, bias_weight, preferred_element_type=F32)  4.57 us

profile of v2, /device:TPU:0, one launch (start us, length us, event | category | flops | bytes accessed | tf_op | source)
XLA Modules:
  0.0 197.8 jit_solution(14719233474083535863)
XLA Ops:
  0.6 0.0 copy-start
  0.6 0.0 copy-start.1
  0.7 0.0 copy-start.8
  0.7 1.9 convert_reduce_fusion
  2.5 0.0 copy-start.4
  2.6 2.8 %fusion.11 = f32[24,192]{1,0:T(8,128)S(1)} fusion(bf16[24,192,128]{2,1,0:T(8,128)(2,1)} %param.6, f32[24,192]{1,0:T(8,128)S(1)} %broadcast_multiply_fusion.2), kind=kLoop, calls=%fused_computation.13 | loop fusion | flops 2354688 | bytes 1216512 | tf_op jit(solution)/shard_map/reduce_sum | solution.py:375
  5.4 0.0 copy-done.1
  5.4 0.0 copy-done.8
  5.4 0.0 copy-start.6
  5.4 1.5 fusion.15
  6.9 0.0 copy-start.2
  6.9 1.8 copy.11
  8.6 0.0 copy-done
  8.6 0.0 copy-start.7
  8.6 2.0 fusion.13
  10.6 0.7 copy.31
  11.3 0.0 copy-done.2
  11.3 1.8 copy.12
  13.0 0.0 copy-done.7
  13.0 0.7 copy_bitcast_fusion.1.w_in_ref
  13.7 0.6 slice_bitcast_fusion.1.w_out_ref
  15.0 152.5 %shard_map.101 = (bf16[16,12,24,128]{3,2,1,0:T(8,128)(2,1)}, bf16[16,12,24,128]{3,2,1,0:T(8,128)(2,1)}, f32[4,24,192]{2,1,0:T(8,128)}, f32[2,2,2,80,128]{4,3,2,1,0:T(8,128)}) custom-call(s32[1]{0:T(128)S(6)} %copy.33.valid_ref, bf16[16,12,24,128]{3,2,1,0:T(8,128)(2,1)} %bitcast.40, bf16[16,12,24,128]{3,2,1,0:T(8,128)(2,1)} %bitcast.41, ...), custom_call_target="tpu_custom_call" | custom-call | tf_op jit(solution)/shard_map/pallas_call | solution.py:299
  167.5 0.9 convert_element_type.23
  168.4 1.4 bitcast_convert_fusion
  169.8 4.6 %fusion.10 = (f32[128]{0:T(128)S(1)}, f32[24,192]{1,0:T(8,128)}, f32[24,192]{1,0:T(8,128)}, f32[24,192,128]{2,1,0:T(8,128)S(1)}) fusion(bf16[24,192,128]{2,1,0:T(8,128)(2,1)S(1)} %copy-done.1, f32[24,192]{1,0:T(8,128)S(1)} %add_rsqrt_fusion, f32[24,192]{1,0:T(8,128)S(1)} %broadcast_multiply_fusion.2, f32[128]{0:T(128)S(1)} %copy-done.8, ...), kind=kOutput, calls=%fused_computation.12 | convolution fusion | flops 10607488 | bytes 6010880 | tf_op jit(solution)/shard_map/hab,ch->abc/dot_general | solution.py:394
  174.4 0.0 copy-done.4
  174.4 0.0 copy-done.6
  174.4 1.8 convolution_bitcast_fusion
  176.2 0.1 pad.2.clone
  176.3 0.7 maximum_maximum_fusion.mine_ref
  176.9 9.7 %shard_map.102 = f32[8,128]{1,0:T(8,128)} custom-call(f32[8,128]{1,0:T(8,128)} %maximum_maximum_fusion.mine_ref), custom_call_target="tpu_custom_call" | custom-call | tf_op jit(solution)/shard_map/pallas_call | solution.py:357
  186.6 1.3 slice_bitcast_fusion.2
  187.9 1.2 slice_bitcast_fusion.3
  189.1 0.8 broadcast_multiply_fusion
  189.8 0.0 copy-start.3
  189.8 6.0 %fusion.9 = f32[24,192,128]{2,1,0:T(8,128)} fusion(bf16[24,192,128]{2,1,0:T(8,128)(2,1)S(1)} %copy-done.1, f32[24,192,128]{2,1,0:T(8,128)S(1)} %get-tuple-element.16, f32[24,192]{1,0:T(8,128)S(1)} %get-tuple-element.17, f32[24,192]{1,0:T(8,128)S(1)} %get-tuple-element.18, f32[128]{0:T(128)S(1)} %copy-done.8, f32[24,192]{1,0:T(8,128)} %copy-done.6, ...), kind=kLoop, calls=%fused_computation.11 | loop fusion | flops 4718592 | bytes 5972480 | tf_op jit(solution)/shard_map/mul | solution.py:407
  195.8 0.0 copy-start.5
  195.8 0.0 copy-done.3
  195.8 1.3 copy.30
  197.1 0.0 copy-done.5
  197.1 0.7 copy.34
  (3 shorter events, 0.0 us)
Async XLA Ops:
  0.6 8.0 %copy-start = (bf16[128,4]{0,1:T(4,128)(2,1)S(1)}, bf16[128,4]{0,1:T(4,128)(2,1)}, u32[]{:S(2)}) copy-start(bf16[128,4]{0,1:T(4,128)(2,1)} %param.9) | copy-start | bytes 3076
  0.6 4.7 %copy-start.1 = (bf16[24,192,128]{2,1,0:T(8,128)(2,1)S(1)}, bf16[24,192,128]{2,1,0:T(8,128)(2,1)}, u32[]{:S(2)}) copy-start(bf16[24,192,128]{2,1,0:T(8,128)(2,1)} %param.6) | copy-start | bytes 3538948
  0.7 4.7 %copy-start.8 = (f32[128]{0:T(128)S(1)}, f32[128]{0:T(128)}, u32[]{:S(2)}) copy-start(f32[128]{0:T(128)} %param.7) | copy-start | bytes 1540
  2.5 171.8 %copy-start.4 = (f32[24,192]{1,0:T(8,128)}, f32[24,192]{1,0:T(8,128)S(1)}, u32[]{:S(2)}) copy-start(f32[24,192]{1,0:T(8,128)S(1)} %broadcast_multiply_fusion.2) | copy-start | bytes 55300
  5.4 169.0 %copy-start.6 = (f32[24,192]{1,0:T(8,128)}, f32[24,192]{1,0:T(8,128)S(1)}, u32[]{:S(2)}) copy-start(f32[24,192]{1,0:T(8,128)S(1)} %add_rsqrt_fusion) | copy-start | bytes 55300
  6.9 4.4 %copy-start.2 = (bf16[24,192,128]{2,1,0:T(8,128)(2,1)S(1)}, bf16[24,192,128]{2,1,0:T(8,128)(2,1)}, u32[]{:S(2)}) copy-start(bf16[24,192,128]{2,1,0:T(8,128)(2,1)} %param.11) | copy-start | bytes 3538948
  8.6 4.4 %copy-start.7 = (bf16[5,128,128]{2,1,0:T(8,128)(2,1)S(1)}, bf16[5,128,128]{2,1,0:T(8,128)(2,1)}, u32[]{:S(2)}) copy-start(bf16[5,128,128]{2,1,0:T(8,128)(2,1)} %param.8) | copy-start | bytes 491524
  189.8 6.0 %copy-start.3 = (bf16[16,12,24,128]{3,2,1,0:T(8,128)(2,1)S(1)}, bf16[16,12,24,128]{3,2,1,0:T(8,128)(2,1)}, u32[]{:S(2)}) copy-start(bf16[16,12,24,128]{3,2,1,0:T(8,128)(2,1)} %get-tuple-element.9) | copy-start | bytes 3538948
  195.8 1.3 copy-start.5

commit v3 on v2

v3 whole, which is shorter than its diff:
```python
import functools

import jax
import jax.numpy as jnp
from jax import lax
from jax.experimental import pallas as pl
from jax.experimental.pallas import tpu as pltpu
from jax.sharding import PartitionSpec as P

EPS = 1e-05
F32 = jnp.float32
BF16 = jnp.bfloat16


def mm(left, right):
    return lax.dot_general(left, right, (((1,), (0,)), ((), ())), preferred_element_type=F32)


def mm_nt(left, right):
    return lax.dot_general(left, right, (((1,), (1,)), ((), ())), preferred_element_type=F32)


MESH = pl.DeviceIdType.MESH
VM = pltpu.VMEM
DMA = pltpu.SemaphoreType.DMA


def place():
    row, col = lax.axis_index("row"), lax.axis_index("col")
    return row, col, row // 4, lax.rem(row // 2, 2), lax.rem(row, 2)


def greet_all():
    row, col = lax.axis_index("row"), lax.axis_index("col")
    n_row, n_col = lax.axis_size("row"), lax.axis_size("col")
    barrier = pltpu.get_barrier_semaphore()

    def greet(i, carry):
        there = (lax.rem(row + i // n_col, n_row), lax.rem(col + lax.rem(i, n_col), n_col))
        pl.semaphore_signal(barrier, inc=1, device_id=there, device_id_type=MESH)
        return carry

    lax.fori_loop(1, n_row * n_col, greet, 0)
    return barrier, n_row * n_col - 1


def push(src, dst, send, recv, where):
    pltpu.make_async_remote_copy(
        src_ref=src, dst_ref=dst, send_sem=send, recv_sem=recv,
        device_id=where, device_id_type=MESH,
    ).start()


def await_bytes(ref, sem):
    pltpu.make_async_copy(ref, ref, sem).wait()


def mates(n_col, mid, col):
    for i in range(1, 2 * n_col):
        yield i - 1, lax.rem(mid + i // n_col, 2), lax.rem(col + i % n_col, n_col)


def norm(x_f):
    average = jnp.mean(x_f, axis=-1, keepdims=True)
    centered = x_f - average
    inverse = lax.rsqrt(jnp.mean(centered * centered, axis=-1, keepdims=True) + EPS)
    return centered * inverse, inverse


def fold_rows(x_f):
    return jnp.sum(x_f.reshape(-1, 8, x_f.shape[-1]), axis=0)


def attend(
    heads, valid_ref, x_ref, cot_ref, gain, w_in_ref, w_out_ref, bias_s, dbias_s, parts_ref, gain_s, att_ref, dn_ref
):
    n_row, tile_rows, channels = x_ref.shape
    rows = n_row * tile_rows
    width = channels // heads
    scale = width ** (-0.5)
    keep_lanes = lax.broadcasted_iota(jnp.int32, (rows, 1), 0) < valid_ref[0]
    x_hat, _ = norm(x_ref[...].astype(F32).reshape(rows, channels))
    x_f = x_hat * gain
    x = x_f.astype(BF16)
    cot = cot_ref[...].astype(F32).reshape(rows, channels).astype(BF16)
    proj = mm(x, w_in_ref[...])
    query = proj[:, :channels].astype(BF16)
    key_f = jnp.where(keep_lanes, proj[:, channels : 2 * channels], 0.0)
    key = key_f.astype(BF16)
    value_f = proj[:, 2 * channels : 3 * channels]
    value = value_f.astype(BF16)
    gate = jax.nn.sigmoid(proj[:, 3 * channels :])
    d_gated = mm_nt(cot, w_out_ref[...])
    d_context_f = d_gated * gate
    d_context = d_context_f.astype(BF16)
    key_t = jnp.transpose(key_f).astype(BF16)
    value_t = jnp.transpose(value_f).astype(BF16)
    lane_head = lax.broadcasted_iota(jnp.int32, (rows, channels), 1) // width
    ctx_parts, dq_parts = [], []
    dk = jnp.zeros((rows, channels), F32)
    dv = jnp.zeros((rows, channels), F32)
    for h in range(heads):
        mine = lane_head == h
        q_h = jnp.where(mine, query, jnp.zeros_like(query))
        dc_h = jnp.where(mine, d_context, jnp.zeros_like(d_context))
        s = mm_nt(key, q_h) * scale + bias_s[h]
        e = jnp.exp(s - jnp.max(s, axis=0, keepdims=True))
        p = e * (1.0 / jnp.sum(e, axis=0, keepdims=True))
        d_p = mm_nt(value, dc_h)
        delta = jnp.sum(p * d_p, axis=0, keepdims=True)
        ds = p * (d_p - delta)
        dbias_s[h] += ds
        p_b = p.astype(BF16)
        ds_b = ds.astype(BF16)
        ctx_parts.append(mm(value_t[h * width : (h + 1) * width], p_b))
        dq_parts.append(mm(key_t[h * width : (h + 1) * width], ds_b))
        dv += mm(p_b, dc_h)
        dk += mm(ds_b, q_h)
    context = jnp.transpose(jnp.concatenate(ctx_parts, axis=0)).astype(BF16).astype(F32)
    dq = (jnp.transpose(jnp.concatenate(dq_parts, axis=0)) * scale).astype(BF16)
    dk = (dk * scale).astype(BF16)
    dv = dv.astype(BF16)
    gated_f = gate * context
    gated = gated_f.astype(BF16)
    att = mm(gated, w_out_ref[...])
    att_ref[...] = att.reshape(n_row, tile_rows, channels).astype(att_ref.dtype)
    d_gate = (d_gated * context * gate * (1.0 - gate)).astype(BF16)
    grads = jnp.concatenate([dq, dk, dv, d_gate], axis=1)
    dn = mm_nt(grads, w_in_ref[...])
    dn_ref[...] = dn.reshape(n_row, tile_rows, channels).astype(dn_ref.dtype)
    gain_s[...] += fold_rows(dn * x_hat)
    x_t = jnp.transpose(x_f).astype(BF16)
    parts_ref[:, : 4 * channels] += mm(x_t, grads)
    gated_t = jnp.transpose(gated_f).astype(BF16)
    parts_ref[:, 4 * channels :] += mm(gated_t, cot)


def layer_kernel(
    heads, valid_ref, pair_ref, x_ref, cot_ref, gain_ref, bwt_ref, proj_ref,
    atto_ref, pgo_ref, sums_ref, small_ref,
    btile, x_hat_s, normed_s, w_in, xc, cc, ball, bias_s, dbias_s, parts_s, gain_s, att_s, dn_s, dno, bterm,
    rbuf, psend, prbuf, zsend, zrecv, parts_c, qr, qs, qp, qz, qzs, small_s, small_g,
    s_fw, r_fw, s_bw, r_bw, s_bo, r_bo, s_bm, r_bm, s_bc, r_bc,
    s_out, r_out, s_mate, r_mate, s_core, r_core, s_ag, r_ag, s_agc, r_agc, s_small, r_small, s_loc,
):
    row, col, outer, mid, core = place()
    n_row, ncols, tile_rows, channels = x_ref.shape
    n_out, n_col = ball.shape[0], ball.shape[3]
    tile_cols = pair_ref.shape[1]
    rows = n_row * tile_rows
    other = (outer * 4 + mid * 2 + 1 - core, col)
    w_out_ref = proj_ref.at[4]
    gain = gain_ref[...]
    barrier, n_others = greet_all()

    def lanes(h):
        return h // 2, slice(h % 2 * tile_cols, (h % 2 + 1) * tile_cols)

    for a in range(tile_rows):
        x_hat, _ = norm(pair_ref[a].astype(F32))
        normed = (x_hat * gain).astype(BF16)
        x_hat_s[a] = x_hat
        normed_s[a] = normed
        bias_a = mm_nt(bwt_ref[...], normed)
        for h in range(heads):
            p, where = lanes(h)
            btile[p, a : a + 1, where] = bias_a[h : h + 1]
    pl.semaphore_wait(barrier, n_others)
    for i in range(1, n_out):
        there = lax.rem(outer + i, n_out) * 4 + mid * 2 + core
        push(btile, ball.at[outer, mid, core, col], s_bo.at[i - 1], r_bo.at[i - 1], (there, col))
    local = [
        pltpu.make_async_copy(btile, ball.at[outer, mid, core, col], s_loc.at[0]),
        pltpu.make_async_copy(x_ref.at[row], xc.at[:, row], s_loc.at[1]),
        pltpu.make_async_copy(cot_ref.at[row], cc.at[:, row], s_loc.at[2]),
    ]
    for copy in local:
        copy.start()

    def send_out(c, carry):
        def peer(i, carry):
            r = lax.rem(row + i, n_row)
            push(x_ref.at[r, c], xc.at[c, row], s_fw.at[0], r_fw.at[0, c], (r, col))
            push(cot_ref.at[r, c], cc.at[c, row], s_fw.at[1], r_fw.at[1, c], (r, col))
            return carry

        return lax.fori_loop(1, n_row, peer, carry)

    def send_back(c, carry):
        def peer(i, carry):
            r = lax.rem(row + i, n_row)
            push(att_s.at[c, r], atto_ref.at[row, c], s_bw.at[0], r_bw.at[0, c], (r, col))
            push(dn_s.at[c, r], dno.at[c, row], s_bw.at[1], r_bw.at[1, c], (r, col))
            return carry

        return lax.fori_loop(1, n_row, peer, carry)

    early = (ncols + 3) // 4
    lax.fori_loop(0, early, send_out, 0)
    dbias_s[...] = jnp.zeros_like(dbias_s)
    parts_s[...] = jnp.zeros_like(parts_s)
    gain_s[...] = jnp.zeros_like(gain_s)
    for m in range(4):
        w_in[:, m * channels : (m + 1) * channels] = proj_ref[m]
    for copy in local:
        copy.wait()
    for i in range(1, n_out):
        await_bytes(btile, s_bo.at[i - 1])
        await_bytes(btile, r_bo.at[i - 1])
    mine = ball.at[:, mid, core, col]
    for i, m, k in mates(n_col, mid, col):
        push(mine, mine, s_bm.at[i], r_bm.at[i], (outer * 4 + m * 2 + core, k))
    lax.fori_loop(early, ncols, send_out, 0)
    for i in range(2 * n_col - 1):
        await_bytes(mine, s_bm.at[i])
        await_bytes(mine, r_bm.at[i])
    half = ball.at[:, :, core]
    push(half, half, s_bc, r_bc, other)
    await_bytes(half, s_bc)
    await_bytes(half, r_bc)
    keep_lanes = lax.broadcasted_iota(jnp.int32, (rows, 1), 0) < valid_ref[0]
    for h in range(heads):
        p, where = lanes(h)
        for k in range(n_col):
            block = ball[:, :, :, k, p].reshape(rows, 2 * tile_cols)[:, where]
            bias_s[h, :, k * tile_cols : (k + 1) * tile_cols] = jnp.where(keep_lanes, block, -1000000000.0)

    held = ncols * 5 // 12

    def column(c, carry):
        await_bytes(xc.at[c, pl.ds(0, n_row - 1)], r_fw.at[0, c])
        await_bytes(cc.at[c, pl.ds(0, n_row - 1)], r_fw.at[1, c])

        @pl.when((c > 0) & (c <= ncols - held))
        def _():
            send_back(c - 1, 0)

        attend(
            heads, valid_ref, xc.at[c], cc.at[c], gain, w_in, w_out_ref,
            bias_s, dbias_s, parts_s, gain_s, att_s.at[c], dn_s.at[c],
        )
        return carry

    lax.fori_loop(0, ncols, column, 0)

    for h in range(heads):
        p, where = lanes(h)
        for k in range(n_col):
            block = dbias_s[h, :, k * tile_cols : (k + 1) * tile_cols]
            ball[:, :, :, k, p, :, where] = block.reshape(n_out, 2, 2, tile_rows, tile_cols)
    slab = parts_c.shape[3]
    for j in range(5 * channels // slab):
        m, lo = j * slab // channels, j * slab % channels
        first = min(slab, channels - lo)
        piece = parts_s[lo : lo + first, m * channels : (m + 1) * channels]
        if first < slab:
            rest = parts_s[: slab - first, (m + 1) * channels : (m + 2) * channels]
            piece = jnp.concatenate([piece, rest], axis=0)
        parts_c[j // (2 * n_col), j // n_col % 2, j % n_col] = piece
    core_moves = [(ball.at[:, :, 1 - core], rbuf), (parts_c.at[1 - core], qr)]
    for i, (src, dst) in enumerate(core_moves):
        push(src, dst, s_core.at[i], r_core.at[i], other)
    local = [
        pltpu.make_async_copy(att_s.at[:, row], atto_ref.at[row], s_loc.at[0]),
        pltpu.make_async_copy(dn_s.at[:, row], dno.at[:, row], s_loc.at[1]),
    ]
    for copy in local:
        copy.start()
    for i, (src, dst) in enumerate(core_moves):
        await_bytes(dst, s_core.at[i])
        await_bytes(dst, r_core.at[i])
    for m in range(2):
        for k in range(n_col):
            psend[m, k] = (ball[:, m, core, k] + rbuf[:, m, k]).astype(BF16)
    qs[...] = parts_c[core] + qr[...]
    for i, m, k in mates(n_col, mid, col):
        push(psend.at[m, k], prbuf.at[i], s_mate.at[0, i], r_mate.at[0, i], (outer * 4 + m * 2 + core, k))
        push(qs.at[m, k], qp.at[i], s_mate.at[1, i], r_mate.at[1, i], (outer * 4 + m * 2 + core, k))
    for i in range(2 * n_col - 1):
        for j, ref in ((0, prbuf.at[i]), (1, qp.at[i])):
            await_bytes(ref, s_mate.at[j, i])
            await_bytes(ref, r_mate.at[j, i])
    own = psend[mid, col].astype(F32)
    mine = qs[mid, col]
    for i in range(2 * n_col - 1):
        own += prbuf[i].astype(F32)
        mine += qp[i]
    zsend[...] = own
    qzs[...] = mine
    for i in range(1, n_out):
        o = lax.rem(outer + i, n_out)
        there = (o * 4 + mid * 2 + core, col)
        push(zsend.at[o], zrecv.at[i - 1], s_out.at[0, i - 1], r_out.at[0, i - 1], there)
        push(qzs, qz.at[i - 1], s_out.at[1, i - 1], r_out.at[1, i - 1], there)
    last = (held + 1) // 2
    lax.fori_loop(ncols - held, ncols - last, send_back, 0)
    for i in range(n_out - 1):
        for j, ref in ((0, zrecv.at[i]), (1, qz.at[i])):
            await_bytes(ref, s_out.at[j, i])
            await_bytes(ref, r_out.at[j, i])
    total, sums = zsend[outer], qzs[...]
    for i in range(n_out - 1):
        total += zrecv[i]
        sums += qz[i]
    sums_ref[core, mid, col] = sums
    mine = sums_ref.at[core, mid, col]
    for i, m, k in mates(n_col, mid, col):
        push(mine, mine, s_ag.at[i], r_ag.at[i], (outer * 4 + m * 2 + core, k))

    btile[...] = total
    no_heads = jnp.zeros((8 - heads, tile_cols), F32)
    weight_part = jnp.zeros((8, channels), F32)
    gain_part = gain_s[...]
    for a in range(tile_rows):
        d_rows = [btile[p, a : a + 1, where] for p, where in map(lanes, range(heads))]
        d_a = jnp.concatenate(d_rows + [no_heads], axis=0).astype(BF16)
        term = lax.dot_general(d_a, bwt_ref[...], (((0,), (0,)), ((), ())), preferred_element_type=F32)
        bterm[pl.ds(a, tile_cols, stride=tile_rows), :] = term
        weight_part += mm(d_a, normed_s[a])
        gain_part += fold_rows(term * x_hat_s[a])
    at = lax.broadcasted_iota(jnp.int32, (8, channels), 0)
    gain_row = jnp.broadcast_to(jnp.sum(gain_part, axis=0, keepdims=True), (8, channels))
    small_s[...] = jnp.where(at < heads, weight_part, jnp.where(at == heads, gain_row, 0.0))

    def spread(i, carry):
        there = (lax.rem(row + i // n_col, n_row), lax.rem(col + lax.rem(i, n_col), n_col))
        push(small_s, small_g.at[i - 1], s_small, r_small, there)
        return carry

    lax.fori_loop(1, n_row * n_col, spread, 0)
    lax.fori_loop(ncols - last, ncols, send_back, 0)
    for copy in local:
        copy.wait()

    def finish(c, carry):
        await_bytes(dno.at[c, pl.ds(0, n_row - 1)], r_bw.at[1, c])
        x_hat, inverse = norm(x_ref[:, c].astype(F32).reshape(rows, channels))
        block = [bterm[pl.ds(pl.multiple_of((r * ncols + c) * tile_rows, 8), tile_rows), :] for r in range(n_row)]
        g = (dno[c].astype(F32).reshape(rows, channels) + jnp.concatenate(block, axis=0)) * gain
        inner = jnp.mean(g * x_hat, axis=-1, keepdims=True)
        out = inverse * (g - jnp.mean(g, axis=-1, keepdims=True) - x_hat * inner)
        pgo_ref[:, c] = out.reshape(n_row, tile_rows, channels)
        return carry

    early = ncols - last
    lax.fori_loop(0, early, finish, 0)
    for i in range(2 * n_col - 1):
        await_bytes(mine, s_ag.at[i])
        await_bytes(mine, r_ag.at[i])
    half = sums_ref.at[core]
    push(half, half, s_agc, r_agc, other)
    lax.fori_loop(early, ncols, finish, 0)
    await_bytes(half, s_agc)
    await_bytes(half, r_agc)
    await_bytes(small_g, s_small)
    await_bytes(small_g, r_small)
    small_ref[...] = small_s[...] + jnp.sum(small_g[...], axis=0)

    def came_back(c, carry):
        await_bytes(att_s.at[c, pl.ds(0, n_row - 1)], r_bw.at[0, c])
        return carry

    lax.fori_loop(0, ncols, came_back, 0)
    for k in range(2):
        await_bytes(x_ref.at[pl.ds(0, n_row - 1)], s_fw.at[k])
        await_bytes(x_ref.at[pl.ds(0, n_row - 1)], s_bw.at[k])


def layer(heads, valid_len, pair, x_tiles, cot_tiles, gain, bias_rows, projections):
    n_row, ncols, tile_rows, channels = x_tiles.shape
    n_col = lax.axis_size("col")
    tile_cols = pair.shape[1]
    tile = (heads // 2, tile_rows, 2 * tile_cols)
    n_out, n_mates, rows = n_row // 4, 2 * n_col - 1, n_row * tile_rows
    slab = (5 * channels // (4 * n_col), channels)
    vmem = pl.BlockSpec(memory_space=VM)
    cols = VM((ncols, n_row, tile_rows, channels), BF16)
    return pl.pallas_call(
        functools.partial(layer_kernel, heads),
        in_specs=[pl.BlockSpec(memory_space=pltpu.SMEM)] + [vmem] * 6,
        out_specs=[vmem] * 4,
        out_shape=[
            jax.ShapeDtypeStruct(x_tiles.shape, BF16),
            jax.ShapeDtypeStruct(x_tiles.shape, F32),
            jax.ShapeDtypeStruct((2, 2, n_col) + slab, F32),
            jax.ShapeDtypeStruct((8, channels), F32),
        ],
        scratch_shapes=[
            VM(tile, F32),
            VM(pair.shape, F32),
            VM(pair.shape, BF16),
            VM((channels, 4 * channels), BF16),
            cols, cols,
            VM((n_out, 2, 2, n_col) + tile, F32),
            VM((heads, rows, rows), F32),
            VM((heads, rows, rows), F32),
            VM((channels, 5 * channels), F32),
            VM((8, channels), F32),
            cols, cols, cols,
            VM((tile_cols * tile_rows, channels), F32),
            VM((n_out, 2, n_col) + tile, F32),
            VM((2, n_col, n_out) + tile, BF16),
            VM((n_mates, n_out) + tile, BF16),
            VM((n_out,) + tile, F32),
            VM((n_out - 1,) + tile, F32),
            VM((2, 2, n_col) + slab, F32),
            VM((2, n_col) + slab, F32),
            VM((2, n_col) + slab, F32),
            VM((n_mates,) + slab, F32),
            VM((n_out - 1,) + slab, F32),
            VM(slab, F32),
            VM((8, channels), F32),
            VM((n_row * n_col - 1, 8, channels), F32),
            DMA((2,)), DMA((2, ncols)), DMA((2,)), DMA((2, ncols)),
            DMA((n_out - 1,)), DMA((n_out - 1,)), DMA((n_mates,)), DMA((n_mates,)), DMA, DMA,
            DMA((2, n_out - 1)), DMA((2, n_out - 1)),
            DMA((2, n_mates)), DMA((2, n_mates)), DMA((2,)), DMA((2,)),
            DMA((n_mates,)), DMA((n_mates,)), DMA, DMA, DMA, DMA, DMA((3,)),
        ],
        compiler_params=pltpu.CompilerParams(
            collective_id=0, has_side_effects=True, vmem_limit_bytes=62 * 1024 * 1024
        ),
    )(valid_len, pair, x_tiles, cot_tiles, gain, bias_rows, projections)


def shards(pair, gain, projections, bias_weight, valid_len, out_cotangent):
    n_row = lax.axis_size("row")
    tile_rows, tile_cols, channels = pair.shape
    heads = bias_weight.shape[1]

    def to_columns(tile):
        return jnp.swapaxes(tile, 0, 1).reshape(n_row, tile_cols // n_row, tile_rows, channels)

    def to_tile(columns):
        return jnp.swapaxes(columns.reshape(tile_cols, tile_rows, channels), 0, 1)

    bias_rows = jnp.pad(bias_weight.T, ((0, 8 - heads), (0, 0)))
    attended, pair_gradient, sums, small = layer(
        heads, valid_len, pair, to_columns(pair), to_columns(out_cotangent), gain[None], bias_rows, projections
    )
    return (
        to_tile(attended),
        to_tile(pair_gradient),
        sums.reshape(5, channels, channels),
        small[:heads].T,
        small[heads],
    )


def solution(mesh):
    placed = (P("row", "col", None), P(), P(), P(), P(), P("row", "col", None))
    return jax.shard_map(
        shards,
        mesh=mesh,
        in_specs=placed,
        out_specs=(P("row", "col", None), P("row", "col", None), P(), P(), P()),
        check_vma=False,
    )
```

time: 198 us -> 161 us (0.81)
  other arithmetic: 15.8 us -> 0 us
  Pallas kernels: 162 us -> 147 us
  matrix products: 8.33 us -> 0 us
  local copies, waits for them, and re-layouts: 10.1 us -> 12.5 us
    pallas_call x1 -> x0, Pallas kernels: 9.68 us -> none  [share(): pl.pallas_call(share_kernel, in_specs=[vmem], out_specs=vmem, out_shape=j...]
    dot_general x3 -> x0, matrix products: 8.33 us -> none  [the longest x1 4.57 us: shards(): jnp.einsum('hab,ch->abc', d_bias, bias_weight, preferred_element_type=F32)]
    mul x1 -> x0, other arithmetic: 5.95 us -> none  [shards(): inverse_deviation * (scaled_output - jnp.mean(scaled_output, axis=-1, kee...]
    pallas_call x1, Pallas kernels: 153 us -> 147 us  [layer(): pl.pallas_call(functools.partial(layer_kernel, heads), in_specs=[pl.Block...]
    reduce_sum x2 -> x0, other arithmetic: 4.64 us -> none  [the longest x1 2.78 us: shards(): var = jnp.mean((pair_float - average_value) ** 2, axis=-1, keepdims=True)]
    reshape x1 -> x2, local copies, waits for them, and re-layouts: 1.28 us -> 4.52 us  [to_tile(): return jnp.swapaxes(columns.reshape(tile_cols, tile_rows, channels), 0, 1)]
    convert_element_type x2 -> x0, other arithmetic: 2.32 us -> none  [the longest x1 1.42 us: shards(): normalized_gradient = to_tile(dn_tile).astype(F32) + bias_term]
where the time goes in v3:
time: 161 us
  Pallas kernels  147 us (91%)
  local copies, waits for them, and re-layouts  12.5 us (8%)
    pallas_call x1, Pallas kernels, layer(): pl.pallas_call(functools.partial(layer_kernel, heads), in_specs=[pl.Block...  147 us
    transpose x2, local copies, waits for them, and re-layouts, to_columns(): jnp.swapaxes(tile, 0, 1)  4.92 us
    reshape x2, local copies, waits for them, and re-layouts, to_tile(): return jnp.swapaxes(columns.reshape(tile_cols, tile_rows, channels), 0, 1)  4.52 us

profile of v3, /device:TPU:0, one launch (start us, length us, event | category | flops | bytes accessed | tf_op | source)
XLA Modules:
  0.0 160.9 jit_solution(2178499034391383037)
XLA Ops:
  1.3 1.3 pad.4.bwt_ref
  2.5 0.0 copy-start
  2.5 3.1 %copy.12 = bf16[192,24,128]{2,1,0:T(8,128)(2,1)} copy(bf16[192,24,128]{2,0,1:T(8,128)(2,1)} %bitcast.24) | data formatting | bytes 2359296 | tf_op jit(solution)/shard_map/transpose | solution.py:432
  5.7 0.0 copy-done
  5.7 1.8 %copy.11 = bf16[192,24,128]{2,1,0:T(8,128)(2,1)} copy(bf16[192,24,128]{2,0,1:T(8,128)(2,1)S(1)} %bitcast.19) | data formatting | bytes 2359296 | tf_op jit(solution)/shard_map/transpose | solution.py:432
  7.5 147.0 %shard_map.101 = (bf16[16,12,24,128]{3,2,1,0:T(8,128)(2,1)}, f32[16,12,24,128]{3,2,1,0:T(8,128)}, f32[2,2,2,80,128]{4,3,2,1,0:T(8,128)}, f32[8,128]{1,0:T(8,128)}) custom-call(s32[1]{0:T(128)S(6)} %copy.20.valid_ref, bf16[24,192,128]{2,1,0:T(8,128)(2,1)} %pair_ref.1, bf16[16,12,24,128]{3,2,1,0:T(8,128)(2,1)} %bitcast.21, bf16[16,12,24,128]{3,2,1,0:T(8,128)(2,1)} %bitcast.20, ...), custom_call_target="tpu_custom_call" | custom-call | tf_op jit(solution)/shard_map/pallas_call | solution.py:378
  154.5 0.0 copy-start.1
  154.5 2.7 %copy.18 = bf16[192,24,128]{2,0,1:T(8,128)(2,1)} copy(bf16[192,24,128]{2,1,0:T(8,128)(2,1)} %bitcast.26) | data formatting | bytes 2359296 | tf_op jit(solution)/shard_map/reshape | solution.py:435
  157.2 0.0 copy-done.1
  157.2 0.0 copy-start.3
  157.2 0.0 copy-start.2
  157.2 1.8 %copy.17 = f32[192,24,128]{2,0,1:T(8,128)} copy(f32[192,24,128]{2,1,0:T(8,128)S(1)} %bitcast.23) | data formatting | bytes 4718592 | tf_op jit(solution)/shard_map/reshape | solution.py:435
  159.0 0.0 copy-done.3
  159.0 0.5 slice_bitcast_fusion.1
  159.6 0.6 slice_bitcast_fusion
  160.1 0.0 copy-done.2
  160.1 0.7 copy.21
Async XLA Ops:
  2.5 3.1 %copy-start = (bf16[24,192,128]{2,1,0:T(8,128)(2,1)S(1)}, bf16[24,192,128]{2,1,0:T(8,128)(2,1)}, u32[]{:S(2)}) copy-start(bf16[24,192,128]{2,1,0:T(8,128)(2,1)} %pair_ref.1) | copy-start | bytes 3538948
  154.5 2.7 %copy-start.1 = (f32[16,12,24,128]{3,2,1,0:T(8,128)S(1)}, f32[16,12,24,128]{3,2,1,0:T(8,128)}, u32[]{:S(2)}) copy-start(f32[16,12,24,128]{3,2,1,0:T(8,128)} %get-tuple-element.10) | copy-start | bytes 7077892
  157.2 1.8 %copy-start.3 = (f32[8,128]{1,0:T(8,128)S(1)}, f32[8,128]{1,0:T(8,128)}, u32[]{:S(2)}) copy-start(f32[8,128]{1,0:T(8,128)} %get-tuple-element.12) | copy-start | bytes 12292
  157.2 2.9 %copy-start.2 = (f32[2,2,2,80,128]{4,3,2,1,0:T(8,128)S(1)}, f32[2,2,2,80,128]{4,3,2,1,0:T(8,128)}, u32[]{:S(2)}) copy-start(f32[2,2,2,80,128]{4,3,2,1,0:T(8,128)} %get-tuple-element.11) | copy-start | bytes 983044

commit v4 on v3

v4 whole, which is shorter than its diff:
```python
import functools

import jax
import jax.numpy as jnp
from jax import lax
from jax.experimental import pallas as pl
from jax.experimental.pallas import tpu as pltpu
from jax.sharding import PartitionSpec as P

EPS = 1e-05
F32 = jnp.float32
BF16 = jnp.bfloat16


def mm(left, right):
    return lax.dot_general(left, right, (((1,), (0,)), ((), ())), preferred_element_type=F32)


def mm_nt(left, right):
    return lax.dot_general(left, right, (((1,), (1,)), ((), ())), preferred_element_type=F32)


MESH = pl.DeviceIdType.MESH
VM = pltpu.VMEM
DMA = pltpu.SemaphoreType.DMA


def place():
    row, col = lax.axis_index("row"), lax.axis_index("col")
    return row, col, row // 4, lax.rem(row // 2, 2), lax.rem(row, 2)


def greet_all():
    row, col = lax.axis_index("row"), lax.axis_index("col")
    n_row, n_col = lax.axis_size("row"), lax.axis_size("col")
    barrier = pltpu.get_barrier_semaphore()

    def greet(i, carry):
        there = (lax.rem(row + i // n_col, n_row), lax.rem(col + lax.rem(i, n_col), n_col))
        pl.semaphore_signal(barrier, inc=1, device_id=there, device_id_type=MESH)
        return carry

    lax.fori_loop(1, n_row * n_col, greet, 0)
    return barrier, n_row * n_col - 1


def push(src, dst, send, recv, where):
    pltpu.make_async_remote_copy(
        src_ref=src, dst_ref=dst, send_sem=send, recv_sem=recv,
        device_id=where, device_id_type=MESH,
    ).start()


def await_bytes(ref, sem):
    pltpu.make_async_copy(ref, ref, sem).wait()


def mates(n_col, mid, col):
    for i in range(1, 2 * n_col):
        yield i - 1, lax.rem(mid + i // n_col, 2), lax.rem(col + i % n_col, n_col)


def norm(x_f):
    average = jnp.mean(x_f, axis=-1, keepdims=True)
    centered = x_f - average
    inverse = lax.rsqrt(jnp.mean(centered * centered, axis=-1, keepdims=True) + EPS)
    return centered * inverse, inverse


def fold_rows(x_f):
    return jnp.sum(x_f.reshape(-1, 8, x_f.shape[-1]), axis=0)


def attend(
    heads, valid_ref, x_ref, cot_ref, gain, w_in_ref, w_out_ref, bias_s, dbias_s, parts_ref, gain_s, att_ref, dn_ref
):
    n_row, tile_rows, channels = x_ref.shape
    rows = n_row * tile_rows
    width = channels // heads
    scale = width ** (-0.5)
    keep_lanes = lax.broadcasted_iota(jnp.int32, (rows, 1), 0) < valid_ref[0]
    x_hat, _ = norm(x_ref[...].astype(F32).reshape(rows, channels))
    x_f = x_hat * gain
    x = x_f.astype(BF16)
    cot = cot_ref[...].astype(F32).reshape(rows, channels).astype(BF16)
    proj = mm(x, w_in_ref[...])
    query = proj[:, :channels].astype(BF16)
    key_f = jnp.where(keep_lanes, proj[:, channels : 2 * channels], 0.0)
    key = key_f.astype(BF16)
    value_f = proj[:, 2 * channels : 3 * channels]
    value = value_f.astype(BF16)
    gate = jax.nn.sigmoid(proj[:, 3 * channels :])
    d_gated = mm_nt(cot, w_out_ref[...])
    d_context_f = d_gated * gate
    d_context = d_context_f.astype(BF16)
    key_t = jnp.transpose(key_f).astype(BF16)
    value_t = jnp.transpose(value_f).astype(BF16)
    lane_head = lax.broadcasted_iota(jnp.int32, (rows, channels), 1) // width
    ctx_parts, dq_parts = [], []
    dk = jnp.zeros((rows, channels), F32)
    dv = jnp.zeros((rows, channels), F32)
    for h in range(heads):
        mine = lane_head == h
        q_h = jnp.where(mine, query, jnp.zeros_like(query))
        dc_h = jnp.where(mine, d_context, jnp.zeros_like(d_context))
        s = mm_nt(key, q_h) * scale + bias_s[h]
        e = jnp.exp(s - jnp.max(s, axis=0, keepdims=True))
        p = e * (1.0 / jnp.sum(e, axis=0, keepdims=True))
        d_p = mm_nt(value, dc_h)
        delta = jnp.sum(p * d_p, axis=0, keepdims=True)
        ds = p * (d_p - delta)
        dbias_s[h] += ds
        p_b = p.astype(BF16)
        ds_b = ds.astype(BF16)
        ctx_parts.append(mm(value_t[h * width : (h + 1) * width], p_b))
        dq_parts.append(mm(key_t[h * width : (h + 1) * width], ds_b))
        dv += mm(p_b, dc_h)
        dk += mm(ds_b, q_h)
    context = jnp.transpose(jnp.concatenate(ctx_parts, axis=0)).astype(BF16).astype(F32)
    dq = (jnp.transpose(jnp.concatenate(dq_parts, axis=0)) * scale).astype(BF16)
    dk = (dk * scale).astype(BF16)
    dv = dv.astype(BF16)
    gated_f = gate * context
    gated = gated_f.astype(BF16)
    att = mm(gated, w_out_ref[...])
    att_ref[...] = att.reshape(n_row, tile_rows, channels).astype(att_ref.dtype)
    d_gate = (d_gated * context * gate * (1.0 - gate)).astype(BF16)
    grads = jnp.concatenate([dq, dk, dv, d_gate], axis=1)
    dn = mm_nt(grads, w_in_ref[...])
    dn_ref[...] = dn.reshape(n_row, tile_rows, channels).astype(dn_ref.dtype)
    gain_s[...] += fold_rows(dn * x_hat)
    x_t = jnp.transpose(x_f).astype(BF16)
    parts_ref[:, : 4 * channels] += mm(x_t, grads)
    gated_t = jnp.transpose(gated_f).astype(BF16)
    parts_ref[:, 4 * channels :] += mm(gated_t, cot)


def layer_kernel(
    heads, valid_ref, pair_ref, cot_ref, gain_ref, bwt_ref, proj_ref,
    atto_ref, pgo_ref, sums_ref, small_ref,
    pair_f, cot_f, x_s, c_s, btile, x_hat_s, normed_s, w_in, xc, cc, ball, bias_s, dbias_s, parts_s, gain_s,
    att_s, dn_s, dno, bterm,
    rbuf, psend, prbuf, zsend, zmate, zopp, zback, parts_c, qr, qs, qp, qmate, qopp, qzs, qhalf, plane_g, outer_g,
    s_fw, r_fw, s_bw, r_bw, s_bo, r_bo, s_bo2, r_bo2, s_bm, r_bm, s_bc, r_bc,
    s_half, r_half, s_opp, r_opp, s_mate, r_mate, s_core, r_core, s_ag, r_ag, s_agc, r_agc,
    s_small, r_small, s_small2, r_small2, s_loc,
):
    row, col, outer, mid, core = place()
    n_row, ncols, tile_rows, channels = x_s.shape
    n_out, n_col = ball.shape[0], ball.shape[3]
    tile_cols = pair_ref.shape[1]
    rows = n_row * tile_rows
    half_out = n_out // 2
    facing = lax.rem(outer + half_out, n_out)
    neighbours = [outer // half_out * half_out + lax.rem(outer + i, half_out) for i in range(1, half_out)]
    other = (outer * 4 + mid * 2 + 1 - core, col)
    w_out_ref = proj_ref.at[4]
    gain = gain_ref[...]

    def along(o):
        return o * 4 + mid * 2 + core, col

    def lanes(h):
        return h // 2, slice(h % 2 * tile_cols, (h % 2 + 1) * tile_cols)

    def turn(c, carry):
        for r in range(n_row):
            at = pl.ds(r * ncols + c, tile_rows, stride=tile_cols)
            x_s[r, c] = pair_f[at, :].astype(BF16)
            c_s[r, c] = cot_f[at, :].astype(BF16)
        return carry

    def send_out(c, carry):
        def peer(i, carry):
            r = lax.rem(row + i, n_row)
            push(x_s.at[r, c], xc.at[c, row], s_fw.at[0], r_fw.at[0, c], (r, col))
            push(c_s.at[r, c], cc.at[c, row], s_fw.at[1], r_fw.at[1, c], (r, col))
            return carry

        return lax.fori_loop(1, n_row, peer, carry)

    def send_back(c, carry):
        def peer(i, carry):
            r = lax.rem(row + i, n_row)
            push(dn_s.at[c, r], dno.at[c, row], s_bw.at[1], r_bw.at[1, c], (r, col))
            push(att_s.at[c, r], atto_ref.at[row, c], s_bw.at[0], r_bw.at[0, c], (r, col))
            return carry

        return lax.fori_loop(1, n_row, peer, carry)

    def turn_and_send(c, carry):
        turn(jnp.minimum(c + 1, ncols - 1), 0)
        return send_out(c, carry)

    barrier, n_others = greet_all()
    for a in range(tile_rows):
        at = slice(a * tile_cols, (a + 1) * tile_cols)
        pair_f[at, :] = pair_ref[a].astype(F32)
        cot_f[at, :] = cot_ref[a].astype(F32)
    lax.fori_loop(0, 2, turn, 0)
    pl.semaphore_wait(barrier, n_others)
    send_out(0, 0)
    for a in range(tile_rows):
        x_hat, _ = norm(pair_f[a * tile_cols : (a + 1) * tile_cols, :])
        normed = (x_hat * gain).astype(BF16)
        x_hat_s[a] = x_hat
        normed_s[a] = normed
        bias_a = mm_nt(bwt_ref[...], normed)
        for h in range(heads):
            p, where = lanes(h)
            btile[p, a : a + 1, where] = bias_a[h : h + 1]
    spot = ball.at[outer, mid, core, col]
    for i, o in enumerate([facing] + neighbours):
        push(btile, spot, s_bo.at[i], r_bo.at[i], along(o))
    own_bias = pltpu.make_async_copy(btile, spot, s_loc.at[0])
    own_bias.start()
    lax.fori_loop(1, 2, turn_and_send, 0)
    dbias_s[...] = jnp.zeros_like(dbias_s)
    for i in range(half_out):
        await_bytes(btile, s_bo.at[i])
        await_bytes(btile, r_bo.at[i])
    spot = ball.at[facing, mid, core, col]
    for i, o in enumerate(neighbours):
        push(spot, spot, s_bo2.at[i], r_bo2.at[i], along(o))
    early = (ncols + 2) // 3
    lax.fori_loop(2, early, turn_and_send, 0)
    own_bias.wait()
    for i in range(half_out - 1):
        await_bytes(spot, s_bo2.at[i])
        await_bytes(spot, r_bo2.at[i])
    mine = ball.at[:, mid, core, col]
    for i, m, k in mates(n_col, mid, col):
        push(mine, mine, s_bm.at[i], r_bm.at[i], (outer * 4 + m * 2 + core, k))
    lax.fori_loop(early, ncols, turn_and_send, 0)
    local = [
        pltpu.make_async_copy(x_s.at[row], xc.at[:, row], s_loc.at[1]),
        pltpu.make_async_copy(c_s.at[row], cc.at[:, row], s_loc.at[2]),
    ]
    for copy in local:
        copy.start()
    parts_s[...] = jnp.zeros_like(parts_s)
    gain_s[...] = jnp.zeros_like(gain_s)
    for m in range(4):
        w_in[:, m * channels : (m + 1) * channels] = proj_ref[m]
    for i in range(2 * n_col - 1):
        await_bytes(mine, s_bm.at[i])
        await_bytes(mine, r_bm.at[i])
    half = ball.at[:, :, core]
    push(half, half, s_bc, r_bc, other)
    await_bytes(half, s_bc)
    await_bytes(half, r_bc)
    for copy in local:
        copy.wait()
    keep_lanes = lax.broadcasted_iota(jnp.int32, (rows, 1), 0) < valid_ref[0]
    for h in range(heads):
        p, where = lanes(h)
        for k in range(n_col):
            block = ball[:, :, :, k, p].reshape(rows, 2 * tile_cols)[:, where]
            bias_s[h, :, k * tile_cols : (k + 1) * tile_cols] = jnp.where(keep_lanes, block, -1000000000.0)

    held = ncols * 1 // 12

    def column(c, carry):
        await_bytes(xc.at[c, pl.ds(0, n_row - 1)], r_fw.at[0, c])
        await_bytes(cc.at[c, pl.ds(0, n_row - 1)], r_fw.at[1, c])

        @pl.when((c > 0) & (c <= ncols - held))
        def _():
            send_back(c - 1, 0)

        attend(
            heads, valid_ref, xc.at[c], cc.at[c], gain, w_in, w_out_ref,
            bias_s, dbias_s, parts_s, gain_s, att_s.at[c], dn_s.at[c],
        )
        return carry

    lax.fori_loop(0, ncols, column, 0)

    n_pairs = heads // 2
    for p in range(n_pairs):
        for h in (2 * p, 2 * p + 1):
            _, where = lanes(h)
            for k in range(n_col):
                block = dbias_s[h, :, k * tile_cols : (k + 1) * tile_cols]
                ball[:, :, :, k, p, :, where] = block.reshape(n_out, 2, 2, tile_rows, tile_cols)
        push(ball.at[:, :, 1 - core, :, p], rbuf.at[p], s_core.at[p], r_core.at[p], other)
    slab = parts_c.shape[3]
    for j in range(5 * channels // slab):
        m, lo = j * slab // channels, j * slab % channels
        first = min(slab, channels - lo)
        piece = parts_s[lo : lo + first, m * channels : (m + 1) * channels]
        if first < slab:
            rest = parts_s[: slab - first, (m + 1) * channels : (m + 2) * channels]
            piece = jnp.concatenate([piece, rest], axis=0)
        parts_c[j // (2 * n_col), j // n_col % 2, j % n_col] = piece
    push(parts_c.at[1 - core], qr, s_core.at[n_pairs], r_core.at[n_pairs], other)
    local = [
        pltpu.make_async_copy(att_s.at[:, row], atto_ref.at[row], s_loc.at[0]),
        pltpu.make_async_copy(dn_s.at[:, row], dno.at[:, row], s_loc.at[1]),
    ]
    for copy in local:
        copy.start()
    for p in range(n_pairs):
        await_bytes(rbuf.at[p], s_core.at[p])
        await_bytes(rbuf.at[p], r_core.at[p])
        for m in range(2):
            for k in range(n_col):
                psend[p, m, k] = (ball[:, m, core, k, p] + rbuf[p, :, m, k]).astype(BF16)
        for i, m, k in mates(n_col, mid, col):
            push(psend.at[p, m, k], prbuf.at[p, i], s_mate.at[p, i], r_mate.at[p, i], (outer * 4 + m * 2 + core, k))
    await_bytes(qr, s_core.at[n_pairs])
    await_bytes(qr, r_core.at[n_pairs])
    qs[...] = parts_c[core] + qr[...]
    for i, m, k in mates(n_col, mid, col):
        push(qs.at[m, k], qp.at[i], s_mate.at[n_pairs, i], r_mate.at[n_pairs, i], (outer * 4 + m * 2 + core, k))
    for p in range(n_pairs):
        own = psend[p, mid, col].astype(F32)
        for i in range(2 * n_col - 1):
            await_bytes(prbuf.at[p, i], s_mate.at[p, i])
            await_bytes(prbuf.at[p, i], r_mate.at[p, i])
            own += prbuf[p, i].astype(F32)
        zsend[:, p] = own
    for i, o in enumerate(neighbours):
        for j, z in enumerate((o, lax.rem(o + half_out, n_out))):
            push(zsend.at[z], zmate.at[i, j], s_half.at[j, i], r_half.at[j, i], along(o))
    mine = qs[mid, col]
    for i in range(2 * n_col - 1):
        await_bytes(qp.at[i], s_mate.at[n_pairs, i])
        await_bytes(qp.at[i], r_mate.at[n_pairs, i])
        mine += qp[i]
    qzs[...] = mine
    for i, o in enumerate(neighbours):
        push(qzs, qmate.at[i], s_half.at[2, i], r_half.at[2, i], along(o))
    first, second = held // 4, (held - held // 4) // 2
    last = held - first - second
    lax.fori_loop(ncols - held, ncols - held + first, send_back, 0)
    total, beyond, sums = zsend[outer], zsend[facing], qzs[...]
    for i in range(half_out - 1):
        for j in range(2):
            await_bytes(zopp, s_half.at[j, i])
            await_bytes(zopp, r_half.at[j, i])
        await_bytes(qzs, s_half.at[2, i])
        await_bytes(qzs, r_half.at[2, i])
        total += zmate[i, 0]
        beyond += zmate[i, 1]
        sums += qmate[i]
    zback[...] = beyond
    qhalf[...] = sums
    push(zback, zopp, s_opp.at[0], r_opp.at[0], along(facing))
    push(qhalf, qopp, s_opp.at[1], r_opp.at[1], along(facing))
    lax.fori_loop(ncols - held + first, ncols - last, send_back, 0)
    for j, ref in ((0, zopp), (1, qopp)):
        await_bytes(ref, s_opp.at[j])
        await_bytes(ref, r_opp.at[j])
    total += zopp[...]
    sums += qopp[...]
    sums_ref[core, mid, col] = sums
    mine = sums_ref.at[core, mid, col]
    for i, m, k in mates(n_col, mid, col):
        push(mine, mine, s_ag.at[i], r_ag.at[i], (outer * 4 + m * 2 + core, k))

    btile[...] = total
    no_heads = jnp.zeros((8 - heads, tile_cols), F32)
    weight_part = jnp.zeros((8, channels), F32)
    gain_part = gain_s[...]
    for a in range(tile_rows):
        d_rows = [btile[p, a : a + 1, where] for p, where in map(lanes, range(heads))]
        d_a = jnp.concatenate(d_rows + [no_heads], axis=0).astype(BF16)
        term = lax.dot_general(d_a, bwt_ref[...], (((0,), (0,)), ((), ())), preferred_element_type=F32)
        bterm[pl.ds(a, tile_cols, stride=tile_rows), :] = term
        weight_part += mm(d_a, normed_s[a])
        gain_part += fold_rows(term * x_hat_s[a])
    at = lax.broadcasted_iota(jnp.int32, (8, channels), 0)
    gain_row = jnp.broadcast_to(jnp.sum(gain_part, axis=0, keepdims=True), (8, channels))
    seat = (mid * n_col + col) * 2 + core
    plane_g[seat] = jnp.where(at < heads, weight_part, jnp.where(at == heads, gain_row, 0.0))
    n_plane = 4 * n_col
    for i in range(1, n_plane):
        there = lax.rem(seat + i, n_plane)
        where = (outer * 4 + there // (2 * n_col) * 2 + lax.rem(there, 2), lax.rem(there // 2, n_col))
        push(plane_g.at[seat], plane_g.at[seat], s_small.at[i - 1], r_small.at[i - 1], where)
    for copy in local:
        copy.wait()

    def finish(c, carry):
        await_bytes(dno.at[c, pl.ds(0, n_row - 1)], r_bw.at[1, c])
        x_hat, inverse = norm(x_s[:, c].astype(F32).reshape(rows, channels))
        block = [bterm[pl.ds(pl.multiple_of((r * ncols + c) * tile_rows, 8), tile_rows), :] for r in range(n_row)]
        g = (dno[c].astype(F32).reshape(rows, channels) + jnp.concatenate(block, axis=0)) * gain
        inner = jnp.mean(g * x_hat, axis=-1, keepdims=True)
        out = inverse * (g - jnp.mean(g, axis=-1, keepdims=True) - x_hat * inner)
        pgo_ref[:, c] = out.reshape(n_row, tile_rows, channels)
        return carry

    lax.fori_loop(0, ncols - held, finish, 0)
    for i in range(n_plane - 1):
        await_bytes(plane_g.at[0], s_small.at[i])
        await_bytes(plane_g.at[0], r_small.at[i])
    outer_g[outer] = jnp.sum(plane_g[...], axis=0)
    for i in range(1, n_out):
        push(outer_g.at[outer], outer_g.at[outer], s_small2.at[i - 1], r_small2.at[i - 1], along(lax.rem(outer + i, n_out)))
    lax.fori_loop(ncols - last, ncols, send_back, 0)
    lax.fori_loop(ncols - held, ncols - last, finish, 0)
    for i in range(2 * n_col - 1):
        await_bytes(mine, s_ag.at[i])
        await_bytes(mine, r_ag.at[i])
    half = sums_ref.at[core]
    push(half, half, s_agc, r_agc, other)
    for i in range(n_out - 1):
        await_bytes(outer_g.at[0], s_small2.at[i])
        await_bytes(outer_g.at[0], r_small2.at[i])
    small_ref[...] = jnp.sum(outer_g[...], axis=0)
    await_bytes(half, s_agc)
    await_bytes(half, r_agc)
    lax.fori_loop(ncols - last, ncols, finish, 0)

    def came_back(c, carry):
        await_bytes(att_s.at[c, pl.ds(0, n_row - 1)], r_bw.at[0, c])
        return carry

    lax.fori_loop(0, ncols, came_back, 0)
    for k in range(2):
        await_bytes(x_s.at[pl.ds(0, n_row - 1)], s_fw.at[k])
        await_bytes(x_s.at[pl.ds(0, n_row - 1)], s_bw.at[k])


def layer(heads, valid_len, pair, cot, gain, bias_rows, projections):
    n_row, n_col = lax.axis_size("row"), lax.axis_size("col")
    tile_rows, tile_cols, channels = pair.shape
    ncols = tile_cols // n_row
    tile = (heads // 2, tile_rows, 2 * tile_cols)
    half_tile = tile[1:]
    n_pairs = heads // 2
    n_out, n_mates, rows = n_row // 4, 2 * n_col - 1, n_row * tile_rows
    half_out = n_out // 2
    slab = (5 * channels // (4 * n_col), channels)
    vmem = pl.BlockSpec(memory_space=VM)
    peers = (n_row, ncols, tile_rows, channels)
    cols = VM((ncols, n_row, tile_rows, channels), BF16)
    flat = VM((tile_rows * tile_cols, channels), F32)
    return pl.pallas_call(
        functools.partial(layer_kernel, heads),
        in_specs=[pl.BlockSpec(memory_space=pltpu.SMEM)] + [vmem] * 5,
        out_specs=[vmem] * 4,
        out_shape=[
            jax.ShapeDtypeStruct(peers, BF16),
            jax.ShapeDtypeStruct(peers, F32),
            jax.ShapeDtypeStruct((2, 2, n_col) + slab, F32),
            jax.ShapeDtypeStruct((8, channels), F32),
        ],
        scratch_shapes=[
            flat, flat, VM(peers, BF16), VM(peers, BF16),
            VM(tile, F32),
            VM(pair.shape, F32),
            VM(pair.shape, BF16),
            VM((channels, 4 * channels), BF16),
            cols, cols,
            VM((n_out, 2, 2, n_col) + tile, F32),
            VM((heads, rows, rows), F32),
            VM((heads, rows, rows), F32),
            VM((channels, 5 * channels), F32),
            VM((8, channels), F32),
            cols, cols, cols,
            flat,
            VM((n_pairs, n_out, 2, n_col) + half_tile, F32),
            VM((n_pairs, 2, n_col, n_out) + half_tile, BF16),
            VM((n_pairs, n_mates, n_out) + half_tile, BF16),
            VM((n_out,) + tile, F32),
            VM((half_out - 1, 2) + tile, F32),
            VM(tile, F32),
            VM(tile, F32),
            VM((2, 2, n_col) + slab, F32),
            VM((2, n_col) + slab, F32),
            VM((2, n_col) + slab, F32),
            VM((n_mates,) + slab, F32),
            VM((half_out - 1,) + slab, F32),
            VM(slab, F32),
            VM(slab, F32),
            VM(slab, F32),
            VM((4 * n_col, 8, channels), F32),
            VM((n_out, 8, channels), F32),
            DMA((2,)), DMA((2, ncols)), DMA((2,)), DMA((2, ncols)),
            DMA((half_out,)), DMA((half_out,)), DMA((half_out - 1,)), DMA((half_out - 1,)),
            DMA((n_mates,)), DMA((n_mates,)), DMA, DMA,
            DMA((3, half_out - 1)), DMA((3, half_out - 1)), DMA((2,)), DMA((2,)),
            DMA((n_pairs + 1, n_mates)), DMA((n_pairs + 1, n_mates)), DMA((n_pairs + 1,)), DMA((n_pairs + 1,)),
            DMA((n_mates,)), DMA((n_mates,)), DMA, DMA,
            DMA((4 * n_col - 1,)), DMA((4 * n_col - 1,)), DMA((n_out - 1,)), DMA((n_out - 1,)), DMA((3,)),
        ],
        compiler_params=pltpu.CompilerParams(
            collective_id=0, has_side_effects=True, vmem_limit_bytes=62 * 1024 * 1024
        ),
    )(valid_len, pair, cot, gain, bias_rows, projections)


def shards(pair, gain, projections, bias_weight, valid_len, out_cotangent):
    tile_rows, tile_cols, channels = pair.shape
    heads = bias_weight.shape[1]

    def to_tile(columns):
        return jnp.swapaxes(columns.reshape(tile_cols, tile_rows, channels), 0, 1)

    bias_rows = jnp.pad(bias_weight.T, ((0, 8 - heads), (0, 0)))
    attended, pair_gradient, sums, small = layer(
        heads, valid_len, pair, out_cotangent, gain[None], bias_rows, projections
    )
    return (
        to_tile(attended),
        to_tile(pair_gradient),
        sums.reshape(5, channels, channels),
        small[:heads].T,
        small[heads],
    )


def solution(mesh):
    placed = (P("row", "col", None), P(), P(), P(), P(), P("row", "col", None))
    return jax.shard_map(
        shards,
        mesh=mesh,
        in_specs=placed,
        out_specs=(P("row", "col", None), P("row", "col", None), P(), P(), P()),
        check_vma=False,
    )
```

time: 161 us -> 150 us (0.932)
  Pallas kernels: 147 us -> 139 us
  local copies, waits for them, and re-layouts: 12.5 us -> 9.34 us
    pallas_call x1, Pallas kernels: 147 us -> 139 us  [layer(): pl.pallas_call(functools.partial(layer_kernel, heads), in_specs=[pl.Block...]
    transpose x2 -> x0, local copies, waits for them, and re-layouts: 4.92 us -> none  [to_columns(): jnp.swapaxes(tile, 0, 1)]
where the time goes in v4:
time: 150 us; the launch traced here: 149 us
  Pallas kernels  139 us (93%)
  local copies, waits for them, and re-layouts  9.34 us (6%)
    pallas_call x1, Pallas kernels, layer(): pl.pallas_call(functools.partial(layer_kernel, heads), in_specs=[pl.Block...  139 us
    reshape x2, local copies, waits for them, and re-layouts, to_tile(): return jnp.swapaxes(columns.reshape(tile_cols, tile_rows, channels), 0, 1)  4.9 us

profile of v4, /device:TPU:0, one launch (start us, length us, event | category | flops | bytes accessed | tf_op | source)
XLA Modules:
  0.0 149.4 jit_solution(1236391493853261911)
XLA Ops:
  0.6 1.3 pad.4.bwt_ref
  2.5 138.7 %shard_map.101 = (bf16[16,12,24,128]{3,2,1,0:T(8,128)(2,1)}, f32[16,12,24,128]{3,2,1,0:T(8,128)}, f32[2,2,2,80,128]{4,3,2,1,0:T(8,128)}, f32[8,128]{1,0:T(8,128)}) custom-call(s32[1]{0:T(128)S(6)} %copy.18.valid_ref, bf16[24,192,128]{2,1,0:T(8,128)(2,1)} %pair_ref.1, bf16[24,192,128]{2,1,0:T(8,128)(2,1)} %cot_ref.1, f32[1,128]{1,0:T(1,128)} %bitcast.21, ...), custom_call_target="tpu_custom_call" | custom-call | tf_op jit(solution)/shard_map/pallas_call | solution.py:441
  141.3 1.3 slice_bitcast_fusion
  142.6 1.2 slice_bitcast_fusion.1
  143.7 0.0 copy-start
  143.7 3.6 %copy.15 = f32[192,24,128]{2,0,1:T(8,128)} copy(f32[192,24,128]{2,1,0:T(8,128)} %bitcast.16) | data formatting | bytes 4718592 | tf_op jit(solution)/shard_map/reshape | solution.py:501
  147.4 0.0 copy-done
  147.4 0.0 copy-start.1
  147.4 1.3 copy.16
  148.7 0.0 copy-done.1
  148.7 0.7 copy.19
Async XLA Ops:
  143.7 3.6 %copy-start = (bf16[16,12,24,128]{3,2,1,0:T(8,128)(2,1)S(1)}, bf16[16,12,24,128]{3,2,1,0:T(8,128)(2,1)}, u32[]{:S(2)}) copy-start(bf16[16,12,24,128]{3,2,1,0:T(8,128)(2,1)} %get-tuple-element.9) | copy-start | bytes 3538948
  147.4 1.3 copy-start.1

commit v5 on v4

v5 whole, which is shorter than its diff:
```python
import functools

import jax
import jax.numpy as jnp
from jax import lax
from jax.experimental import pallas as pl
from jax.experimental.pallas import tpu as pltpu
from jax.sharding import PartitionSpec as P

EPS = 1e-05
LOG2E = 1.4426950408889634
F32 = jnp.float32
BF16 = jnp.bfloat16


def mm(left, right):
    return lax.dot_general(left, right, (((1,), (0,)), ((), ())), preferred_element_type=F32)


def mm_nt(left, right):
    return lax.dot_general(left, right, (((1,), (1,)), ((), ())), preferred_element_type=F32)


MESH = pl.DeviceIdType.MESH
VM = pltpu.VMEM
DMA = pltpu.SemaphoreType.DMA


def place():
    row, col = lax.axis_index("row"), lax.axis_index("col")
    return row, col, row // 4, lax.rem(row // 2, 2), lax.rem(row, 2)


def greet_all():
    row, col = lax.axis_index("row"), lax.axis_index("col")
    n_row, n_col = lax.axis_size("row"), lax.axis_size("col")
    barrier = pltpu.get_barrier_semaphore()

    def greet(i, carry):
        there = (lax.rem(row + i // n_col, n_row), lax.rem(col + lax.rem(i, n_col), n_col))
        pl.semaphore_signal(barrier, inc=1, device_id=there, device_id_type=MESH)
        return carry

    lax.fori_loop(1, n_row * n_col, greet, 0)
    return barrier, n_row * n_col - 1


def push(src, dst, send, recv, where):
    pltpu.make_async_remote_copy(
        src_ref=src, dst_ref=dst, send_sem=send, recv_sem=recv,
        device_id=where, device_id_type=MESH,
    ).start()


def await_bytes(ref, sem):
    pltpu.make_async_copy(ref, ref, sem).wait()


def mates(n_col, mid, col):
    for i in range(1, 2 * n_col):
        yield i - 1, lax.rem(mid + i // n_col, 2), lax.rem(col + i % n_col, n_col)


def norm(x_f):
    average = jnp.mean(x_f, axis=-1, keepdims=True)
    centered = x_f - average
    inverse = lax.rsqrt(jnp.mean(centered * centered, axis=-1, keepdims=True) + EPS)
    return centered * inverse, inverse


def fold_rows(x_f):
    return jnp.sum(x_f.reshape(-1, 8, x_f.shape[-1]), axis=0)


def prepare(heads, valid_ref, col_ref, gain, w_in_ref, w_out_ref):
    n_row, _, tile_rows, channels = col_ref.shape
    rows = n_row * tile_rows
    keep_lanes = lax.broadcasted_iota(jnp.int32, (rows, 1), 0) < valid_ref[0]
    x_hat, _ = norm(col_ref[:, 0].astype(F32).reshape(rows, channels))
    x_f = x_hat * gain
    cot = col_ref[:, 1].astype(F32).reshape(rows, channels).astype(BF16)
    proj = mm(x_f.astype(BF16), w_in_ref[...])
    query = proj[:, :channels].astype(BF16)
    key_f = jnp.where(keep_lanes, proj[:, channels : 2 * channels], 0.0)
    value_f = proj[:, 2 * channels : 3 * channels]
    gate = jax.nn.sigmoid(proj[:, 3 * channels :])
    d_gated = mm_nt(cot, w_out_ref[...])
    d_context = (d_gated * gate).astype(BF16)
    return x_hat, x_f, cot, query, key_f, value_f, gate, d_gated, d_context


def attend(heads, chosen, query, key_f, value_f, d_context, bias_s, dbias_s):
    rows, channels = query.shape
    width = channels // heads
    scale = width ** (-0.5)
    key, value = key_f.astype(BF16), value_f.astype(BF16)
    key_t = jnp.transpose(key_f).astype(BF16)
    value_t = jnp.transpose(value_f).astype(BF16)
    lane_head = lax.broadcasted_iota(jnp.int32, (rows, channels), 1) // width
    ctx_parts, dq_parts = [], []
    dk = jnp.zeros((rows, channels), F32)
    dv = jnp.zeros((rows, channels), F32)
    for h in chosen:
        mine = lane_head == h
        q_h = jnp.where(mine, query, jnp.zeros_like(query))
        dc_h = jnp.where(mine, d_context, jnp.zeros_like(d_context))
        s = mm_nt(key, q_h) * (scale * LOG2E) + bias_s[h]
        e = jnp.exp2(s - jnp.max(s, axis=0, keepdims=True))
        p = e * (1.0 / jnp.sum(e, axis=0, keepdims=True))
        d_p = mm_nt(value, dc_h)
        delta = jnp.sum(p * d_p, axis=0, keepdims=True)
        ds = p * (d_p - delta)
        dbias_s[h] += ds
        p_b = p.astype(BF16)
        ds_b = ds.astype(BF16)
        ctx_parts.append(mm(value_t[h * width : (h + 1) * width], p_b))
        dq_parts.append(mm(key_t[h * width : (h + 1) * width], ds_b))
        dv += mm(p_b, dc_h)
        dk += mm(ds_b, q_h)
    ctx_t = jnp.concatenate(ctx_parts, axis=0)
    dq_t = jnp.concatenate(dq_parts, axis=0)
    return ctx_t, dq_t, (dk * scale).astype(BF16), dv.astype(BF16)


def conclude(
    heads, x_hat, x_f, cot, gate, d_gated, ctx_t, dq_t, dk, dv,
    w_in_ref, w_out_ref, parts_ref, gain_s, back_ref,
):
    n_row, _, tile_rows, channels = back_ref.shape
    scale = (channels // heads) ** (-0.5)
    context = jnp.transpose(ctx_t).astype(BF16).astype(F32)
    dq = (jnp.transpose(dq_t) * scale).astype(BF16)
    gated_f = gate * context
    gated = gated_f.astype(BF16)
    att = mm(gated, w_out_ref[...])
    back_ref[:, 1] = att.reshape(n_row, tile_rows, channels).astype(BF16)
    d_gate = (d_gated * context * gate * (1.0 - gate)).astype(BF16)
    grads = jnp.concatenate([dq, dk, dv, d_gate], axis=1)
    dn = mm_nt(grads, w_in_ref[...])
    back_ref[:, 0] = dn.reshape(n_row, tile_rows, channels).astype(BF16)
    gain_s[...] += fold_rows(dn * x_hat)
    x_t = jnp.transpose(x_f).astype(BF16)
    parts_ref[:, : 4 * channels] += mm(x_t, grads)
    gated_t = jnp.transpose(gated_f).astype(BF16)
    parts_ref[:, 4 * channels :] += mm(gated_t, cot)


def layer_kernel(
    heads, valid_ref, pair_ref, cot_ref, gain_ref, bwt_ref, proj_ref,
    atto_ref, pgo_ref, sums_ref, small_ref,
    pair_f, cot_f, x_s, btile, x_hat_s, normed_s, w_in, xc, ball, bias_s, dbias_s, parts_s, gain_s,
    back_s, back, bterm,
    rbuf, psend, prbuf, zsend, zmate, zown, zback, zopp, parts_c, qr, qs, qp, qzs, qmate, qhalf, qopp, plane_g, outer_g,
    s_fw, r_fw, s_bw, r_bw, s_ba, r_ba, s_bb, r_bb, s_by, r_by, s_bx, r_bx, s_bc, r_bc, s_loc,
    s_core, r_core, s_mate, r_mate, s_half, r_half, s_opp, r_opp, s_ag, r_ag, s_agc, r_agc,
    s_small, r_small, s_small2, r_small2,
):
    row, col, outer, mid, core = place()
    n_row, ncols, _, tile_rows, channels = x_s.shape
    n_out, n_col = ball.shape[1], ball.shape[4]
    tile_cols = pair_ref.shape[1]
    rows = n_row * tile_rows
    half_out = n_out // 2
    facing = lax.rem(outer + half_out, n_out)
    neighbours = [outer // half_out * half_out + lax.rem(outer + i, half_out) for i in range(1, half_out)]
    n_near, n_mates = half_out - 1, 2 * n_col - 1
    other = (outer * 4 + mid * 2 + 1 - core, col)
    w_out_ref = proj_ref.at[4]
    gain = gain_ref[...]
    group = heads // 2

    def along(o):
        return o * 4 + mid * 2 + core, col

    def mate(m, k):
        return outer * 4 + m * 2 + core, k

    def members(g):
        for n in range(group):
            yield g * group + n, slice(n * tile_cols, (n + 1) * tile_cols)

    def both(ref, send, recv):
        await_bytes(ref, send)
        await_bytes(ref, recv)

    def turn(c, carry):
        for r in range(n_row):
            at = pl.ds(r * ncols + c, tile_rows, stride=tile_cols)
            x_s[r, c, 0] = pair_f[at, :].astype(BF16)
            x_s[r, c, 1] = cot_f[at, :].astype(BF16)
        return carry

    def send_out(c, carry):
        def peer(i, carry):
            r = lax.rem(row + i, n_row)
            push(x_s.at[r, c], xc.at[c, row], s_fw, r_fw.at[0, c], (r, col))
            return carry

        lax.fori_loop(1, n_row, peer, carry)
        pltpu.make_async_copy(x_s.at[row, c], xc.at[c, row], r_fw.at[1, c]).start()
        return carry

    def send_back(c, carry):
        def peer(i, carry):
            r = lax.rem(row + i, n_row)
            push(back_s.at[c, r], back.at[c, row], s_bw, r_bw.at[0, c], (r, col))
            return carry

        lax.fori_loop(1, n_row, peer, carry)
        pltpu.make_async_copy(back_s.at[c, row], back.at[c, row], r_bw.at[1, c]).start()
        return carry

    def send_some_out(lo, hi):
        def one(c, carry):
            turn(jnp.minimum(c + 1, ncols - 1), 0)
            return send_out(c, carry)

        lax.fori_loop(min(lo, ncols), min(hi, ncols), one, 0)

    def bias_facing(g):
        for i, o in enumerate([facing] + neighbours):
            push(btile.at[g], ball.at[g, outer, mid, core, col], s_ba.at[g, i], r_ba.at[g, i], along(o))
        pltpu.make_async_copy(btile.at[g], ball.at[g, outer, mid, core, col], s_loc.at[g]).start()

    def bias_relay(g):
        for i in range(half_out):
            both(btile.at[g], s_ba.at[g, i], r_ba.at[g, i])
        spot = ball.at[g, facing, mid, core, col]
        for i, o in enumerate(neighbours):
            push(spot, spot, s_bb.at[g, i], r_bb.at[g, i], along(o))

    def bias_mid(g):
        await_bytes(btile.at[g], s_loc.at[g])
        for i in range(n_near):
            both(btile.at[g], s_bb.at[g, i], r_bb.at[g, i])
        mine = ball.at[g, :, mid, core, col]
        push(mine, mine, s_by.at[g], r_by.at[g], mate(1 - mid, col))

    def bias_col(g):
        both(ball.at[g, :, mid, core, col], s_by.at[g], r_by.at[g])
        mine = ball.at[g, :, :, core, col]
        for i in range(1, n_col):
            push(mine, mine, s_bx.at[g, i - 1], r_bx.at[g, i - 1], mate(mid, lax.rem(col + i, n_col)))

    def bias_core(g):
        for i in range(n_col - 1):
            both(ball.at[g, :, :, core, col], s_bx.at[g, i], r_bx.at[g, i])
        mine = ball.at[g, :, :, core]
        push(mine, mine, s_bc.at[g], r_bc.at[g], other)

    def bias_done(g):
        both(ball.at[g, :, :, core], s_bc.at[g], r_bc.at[g])
        keep_lanes = lax.broadcasted_iota(jnp.int32, (rows, 1), 0) < valid_ref[0]
        for h, where in members(g):
            for k in range(n_col):
                block = ball[g, :, :, :, k].reshape(rows, group * tile_cols)[:, where]
                bias_s[h, :, k * tile_cols : (k + 1) * tile_cols] = jnp.where(
                    keep_lanes, block * LOG2E, -1000000000.0
                )

    def dbias_core(g):
        for h, where in members(g):
            for k in range(n_col):
                block = dbias_s[h, :, k * tile_cols : (k + 1) * tile_cols]
                ball[g, :, :, :, k, :, where] = block.reshape(n_out, 2, 2, tile_rows, tile_cols)
        push(ball.at[g, :, :, 1 - core], rbuf.at[g], s_core.at[g], r_core.at[g], other)

    def dbias_plane(g):
        both(rbuf.at[g], s_core.at[g], r_core.at[g])
        for m in range(2):
            for k in range(n_col):
                psend[g, m, k] = (ball[g, :, m, core, k] + rbuf[g, :, m, k]).astype(BF16)
        for i, m, k in mates(n_col, mid, col):
            push(psend.at[g, m, k], prbuf.at[g, i], s_mate.at[g, i], r_mate.at[g, i], mate(m, k))

    def dbias_half(g):
        own = psend[g, mid, col].astype(F32)
        for i in range(n_mates):
            both(prbuf.at[g, i], s_mate.at[g, i], r_mate.at[g, i])
            own += prbuf[g, i].astype(F32)
        zsend[g] = own
        for i, o in enumerate(neighbours):
            for j, z in enumerate((o, lax.rem(o + half_out, n_out))):
                push(zsend.at[g, z], zmate.at[g, i, j], s_half.at[g, j, i], r_half.at[g, j, i], along(o))

    def dbias_facing(g):
        total, beyond = zsend[g, outer], zsend[g, facing]
        for i in range(n_near):
            for j in range(2):
                both(zown.at[g], s_half.at[g, j, i], r_half.at[g, j, i])
            total += zmate[g, i, 0]
            beyond += zmate[g, i, 1]
        zown[g] = total
        zback[g] = beyond
        push(zback.at[g], zopp.at[g], s_opp.at[g], r_opp.at[g], along(facing))

    def dbias_done(g):
        both(zopp.at[g], s_opp.at[g], r_opp.at[g])
        btile[g] = zown[g] + zopp[g]

    def parts_core():
        slab = parts_c.shape[3]
        for j in range(5 * channels // slab):
            m, lo = j * slab // channels, j * slab % channels
            first = min(slab, channels - lo)
            piece = parts_s[lo : lo + first, m * channels : (m + 1) * channels]
            if first < slab:
                rest = parts_s[: slab - first, (m + 1) * channels : (m + 2) * channels]
                piece = jnp.concatenate([piece, rest], axis=0)
            parts_c[j // (2 * n_col), j // n_col % 2, j % n_col] = piece
        push(parts_c.at[1 - core], qr, s_core.at[2], r_core.at[2], other)

    def parts_plane():
        both(qr, s_core.at[2], r_core.at[2])
        qs[...] = parts_c[core] + qr[...]
        for i, m, k in mates(n_col, mid, col):
            push(qs.at[m, k], qp.at[i], s_mate.at[2, i], r_mate.at[2, i], mate(m, k))

    def parts_half():
        mine = qs[mid, col]
        for i in range(n_mates):
            both(qp.at[i], s_mate.at[2, i], r_mate.at[2, i])
            mine += qp[i]
        qzs[...] = mine
        for i, o in enumerate(neighbours):
            push(qzs, qmate.at[i], s_half.at[2, 0, i], r_half.at[2, 0, i], along(o))

    def parts_facing():
        mine = qzs[...]
        for i in range(n_near):
            both(qzs, s_half.at[2, 0, i], r_half.at[2, 0, i])
            mine += qmate[i]
        qhalf[...] = mine
        push(qhalf, qopp, s_opp.at[2], r_opp.at[2], along(facing))

    def parts_back():
        both(qopp, s_opp.at[2], r_opp.at[2])
        sums_ref[core, mid, col] = qhalf[...] + qopp[...]
        mine = sums_ref.at[core, mid, col]
        for i, m, k in mates(n_col, mid, col):
            push(mine, mine, s_ag.at[i], r_ag.at[i], mate(m, k))

    def parts_back_core():
        for i in range(n_mates):
            both(sums_ref.at[core, mid, col], s_ag.at[i], r_ag.at[i])
        push(sums_ref.at[core], sums_ref.at[core], s_agc, r_agc, other)

    barrier, n_others = greet_all()
    for a in range(tile_rows):
        at = slice(a * tile_cols, (a + 1) * tile_cols)
        pair_f[at, :] = pair_ref[a].astype(F32)
        cot_f[at, :] = cot_ref[a].astype(F32)
    for a in range(tile_rows):
        x_hat, _ = norm(pair_f[a * tile_cols : (a + 1) * tile_cols, :])
        normed = (x_hat * gain).astype(BF16)
        x_hat_s[a] = x_hat
        normed_s[a] = normed
        bias_a = mm_nt(bwt_ref[...], normed)
        for g in range(2):
            for h, where in members(g):
                btile[g, a : a + 1, where] = bias_a[h : h + 1]
    pl.semaphore_wait(barrier, n_others)
    bias_facing(0)
    bias_facing(1)
    turn(0, 0)
    bias_relay(0)
    send_some_out(0, 1)
    bias_relay(1)
    send_some_out(1, 2)
    dbias_s[...] = jnp.zeros_like(dbias_s)
    parts_s[...] = jnp.zeros_like(parts_s)
    gain_s[...] = jnp.zeros_like(gain_s)
    for m in range(4):
        w_in[:, m * channels : (m + 1) * channels] = proj_ref[m]
    bias_mid(0)
    send_some_out(2, 3)
    bias_col(0)
    bias_mid(1)
    send_some_out(3, 5)
    bias_col(1)
    send_some_out(5, ncols)
    bias_core(0)
    bias_core(1)
    bias_done(0)
    bias_done(1)

    def step_of(t, carry):
        await_bytes(xc.at[t, pl.ds(0, n_row - 1)], r_fw.at[0, t])
        await_bytes(xc.at[t, 0], r_fw.at[1, t])

        @pl.when((t > 0) & (t < ncols - 1))
        def _():
            send_back(t - 1, 0)

        x_hat, x_f, cot, query, key_f, value_f, gate, d_gated, d_context = prepare(
            heads, valid_ref, xc.at[t], gain, w_in, w_out_ref
        )
        ctx_t, dq_t, dk, dv = attend(heads, range(heads), query, key_f, value_f, d_context, bias_s, dbias_s)
        conclude(
            heads, x_hat, x_f, cot, gate, d_gated, ctx_t, dq_t, dk, dv,
            w_in, w_out_ref, parts_s, gain_s, back_s.at[t],
        )
        return carry

    lax.fori_loop(0, ncols, step_of, 0)

    def arrive(c, carry):
        await_bytes(back.at[c, pl.ds(0, n_row - 1)], r_bw.at[0, c])
        await_bytes(back.at[c, 0], r_bw.at[1, c])
        return carry

    dbias_core(0)
    dbias_core(1)
    parts_core()
    dbias_plane(0)
    dbias_plane(1)
    parts_plane()
    dbias_half(0)
    dbias_half(1)
    parts_half()
    send_back(ncols - 2, 0)
    dbias_facing(0)
    dbias_facing(1)
    parts_facing()
    send_back(ncols - 1, 0)
    dbias_done(0)
    dbias_done(1)
    parts_back()

    no_heads = jnp.zeros((8 - heads, tile_cols), F32)
    weight_part = jnp.zeros((8, channels), F32)
    gain_part = gain_s[...]
    for a in range(tile_rows):
        d_rows = [btile[g, a : a + 1, where] for g in range(2) for _, where in members(g)]
        d_a = jnp.concatenate(d_rows + [no_heads], axis=0).astype(BF16)
        term = lax.dot_general(d_a, bwt_ref[...], (((0,), (0,)), ((), ())), preferred_element_type=F32)
        bterm[pl.ds(a, tile_cols, stride=tile_rows), :] = term
        weight_part += mm(d_a, normed_s[a])
        gain_part += fold_rows(term * x_hat_s[a])
    at = lax.broadcasted_iota(jnp.int32, (8, channels), 0)
    gain_row = jnp.broadcast_to(jnp.sum(gain_part, axis=0, keepdims=True), (8, channels))
    seat = (mid * n_col + col) * 2 + core
    plane_g[seat] = jnp.where(at < heads, weight_part, jnp.where(at == heads, gain_row, 0.0))
    n_plane = 4 * n_col
    for i in range(1, n_plane):
        there = lax.rem(seat + i, n_plane)
        where = (outer * 4 + there // (2 * n_col) * 2 + lax.rem(there, 2), lax.rem(there // 2, n_col))
        push(plane_g.at[seat], plane_g.at[seat], s_small.at[i - 1], r_small.at[i - 1], where)

    def finish(c, carry):
        x_hat, inverse = norm(x_s[:, c, 0].astype(F32).reshape(rows, channels))
        block = [bterm[pl.ds(pl.multiple_of((r * ncols + c) * tile_rows, 8), tile_rows), :] for r in range(n_row)]
        g = (back[c, :, 0].astype(F32).reshape(rows, channels) + jnp.concatenate(block, axis=0)) * gain
        inner = jnp.mean(g * x_hat, axis=-1, keepdims=True)
        out = inverse * (g - jnp.mean(g, axis=-1, keepdims=True) - x_hat * inner)
        pgo_ref[:, c] = out.reshape(n_row, tile_rows, channels)
        atto_ref[:, c] = back[c, :, 1]
        return carry

    def arrive_and_finish(c, carry):
        return finish(c, arrive(c, carry))

    lax.fori_loop(0, ncols // 3, arrive_and_finish, 0)
    for i in range(n_plane - 1):
        both(plane_g.at[0], s_small.at[i], r_small.at[i])
    outer_g[outer] = jnp.sum(plane_g[...], axis=0)
    for i in range(1, n_out):
        push(outer_g.at[outer], outer_g.at[outer], s_small2.at[i - 1], r_small2.at[i - 1], along(lax.rem(outer + i, n_out)))
    parts_back_core()
    lax.fori_loop(ncols // 3, ncols, arrive_and_finish, 0)
    for i in range(n_out - 1):
        both(outer_g.at[0], s_small2.at[i], r_small2.at[i])
    small_ref[...] = jnp.sum(outer_g[...], axis=0)
    both(sums_ref.at[core], s_agc, r_agc)
    await_bytes(x_s.at[pl.ds(0, n_row - 1)], s_fw)
    await_bytes(x_s.at[pl.ds(0, n_row - 1)], s_bw)


def layer(heads, valid_len, pair, cot, gain, bias_rows, projections):
    n_row, n_col = lax.axis_size("row"), lax.axis_size("col")
    tile_rows, tile_cols, channels = pair.shape
    ncols = tile_cols // n_row
    tile = (tile_rows, heads // 2 * tile_cols)
    n_out, n_mates, rows = n_row // 4, 2 * n_col - 1, n_row * tile_rows
    half_out = n_out // 2
    slab = (5 * channels // (4 * n_col), channels)
    vmem = pl.BlockSpec(memory_space=VM)
    peers = (n_row, ncols, tile_rows, channels)
    cols = VM((ncols, n_row, 2, tile_rows, channels), BF16)
    flat = VM((tile_rows * tile_cols, channels), F32)

    def pairs(*shape):
        return [DMA(shape), DMA(shape)]

    return pl.pallas_call(
        functools.partial(layer_kernel, heads),
        in_specs=[pl.BlockSpec(memory_space=pltpu.SMEM)] + [vmem] * 5,
        out_specs=[vmem] * 4,
        out_shape=[
            jax.ShapeDtypeStruct(peers, BF16),
            jax.ShapeDtypeStruct(peers, F32),
            jax.ShapeDtypeStruct((2, 2, n_col) + slab, F32),
            jax.ShapeDtypeStruct((8, channels), F32),
        ],
        scratch_shapes=[
            flat, flat, VM((n_row, ncols, 2, tile_rows, channels), BF16),
            VM((2,) + tile, F32),
            VM(pair.shape, F32),
            VM(pair.shape, BF16),
            VM((channels, 4 * channels), BF16),
            cols,
            VM((2, n_out, 2, 2, n_col) + tile, F32),
            VM((heads, rows, rows), F32),
            VM((heads, rows, rows), F32),
            VM((channels, 5 * channels), F32),
            VM((8, channels), F32),
            cols, cols,
            flat,
            VM((2, n_out, 2, n_col) + tile, F32),
            VM((2, 2, n_col, n_out) + tile, BF16),
            VM((2, n_mates, n_out) + tile, BF16),
            VM((2, n_out) + tile, F32),
            VM((2, half_out - 1, 2) + tile, F32),
            VM((2,) + tile, F32),
            VM((2,) + tile, F32),
            VM((2,) + tile, F32),
            VM((2, 2, n_col) + slab, F32),
            VM((2, n_col) + slab, F32),
            VM((2, n_col) + slab, F32),
            VM((n_mates,) + slab, F32),
            VM(slab, F32),
            VM((half_out - 1,) + slab, F32),
            VM(slab, F32),
            VM(slab, F32),
            VM((4 * n_col, 8, channels), F32),
            VM((n_out, 8, channels), F32),
            DMA, DMA((2, ncols)), DMA, DMA((2, ncols)),
            *pairs(2, half_out), *pairs(2, half_out - 1), *pairs(2), *pairs(2, n_col - 1), *pairs(2), DMA((2,)),
            *pairs(3), *pairs(3, n_mates), *pairs(3, 2, half_out - 1), *pairs(3),
            *pairs(n_mates), DMA, DMA, *pairs(4 * n_col - 1), *pairs(n_out - 1),
        ],
        compiler_params=pltpu.CompilerParams(
            collective_id=0, has_side_effects=True, vmem_limit_bytes=63 * 1024 * 1024
        ),
    )(valid_len, pair, cot, gain, bias_rows, projections)


def shards(pair, gain, projections, bias_weight, valid_len, out_cotangent):
    tile_rows, tile_cols, channels = pair.shape
    heads = bias_weight.shape[1]

    def to_tile(columns):
        return jnp.swapaxes(columns.reshape(tile_cols, tile_rows, channels), 0, 1)

    bias_rows = jnp.pad(bias_weight.T, ((0, 8 - heads), (0, 0)))
    attended, pair_gradient, sums, small = layer(
        heads, valid_len, pair, out_cotangent, gain[None], bias_rows, projections
    )
    return (
        to_tile(attended),
        to_tile(pair_gradient),
        sums.reshape(5, channels, channels),
        small[:heads].T,
        small[heads],
    )


def solution(mesh):
    placed = (P("row", "col", None), P(), P(), P(), P(), P("row", "col", None))
    return jax.shard_map(
        shards,
        mesh=mesh,
        in_specs=placed,
        out_specs=(P("row", "col", None), P("row", "col", None), P(), P(), P()),
        check_vma=False,
    )
```

time: 150 us -> 144 us (0.960)
  Pallas kernels: 139 us -> 133 us
    pallas_call x1, Pallas kernels: 139 us -> 133 us  [layer(): pl.pallas_call(functools.partial(layer_kernel, heads), in_specs=[pl.Block...]
where the time goes in v5:
time: 144 us
  Pallas kernels  133 us (92%)
  local copies, waits for them, and re-layouts  9.34 us (6%)
    pallas_call x1, Pallas kernels, layer(): pl.pallas_call(functools.partial(layer_kernel, heads), in_specs=[pl.Block...  133 us
    reshape x2, local copies, waits for them, and re-layouts, to_tile(): return jnp.swapaxes(columns.reshape(tile_cols, tile_rows, channels), 0, 1)  4.9 us

profile of v5, /device:TPU:0, one launch (start us, length us, event | category | flops | bytes accessed | tf_op | source)
XLA Modules:
  0.0 143.9 jit_solution(15891355567454036203)
XLA Ops:
  0.6 1.3 pad.4.bwt_ref
  2.5 133.3 %shard_map.101 = (bf16[16,12,24,128]{3,2,1,0:T(8,128)(2,1)}, f32[16,12,24,128]{3,2,1,0:T(8,128)}, f32[2,2,2,80,128]{4,3,2,1,0:T(8,128)}, f32[8,128]{1,0:T(8,128)}) custom-call(s32[1]{0:T(128)S(6)} %copy.18.valid_ref, bf16[24,192,128]{2,1,0:T(8,128)(2,1)} %pair_ref.1, bf16[24,192,128]{2,1,0:T(8,128)(2,1)} %cot_ref.1, f32[1,128]{1,0:T(1,128)} %bitcast.21, ...), custom_call_target="tpu_custom_call" | custom-call | tf_op jit(solution)/shard_map/pallas_call | solution.py:495
  135.8 1.3 slice_bitcast_fusion
  137.1 1.2 slice_bitcast_fusion.1
  138.3 0.0 copy-start
  138.3 3.6 %copy.15 = f32[192,24,128]{2,0,1:T(8,128)} copy(f32[192,24,128]{2,1,0:T(8,128)} %bitcast.16) | data formatting | bytes 4718592 | tf_op jit(solution)/shard_map/reshape | solution.py:553
  141.9 0.0 copy-done
  141.9 0.0 copy-start.1
  141.9 1.3 copy.16
  143.2 0.0 copy-done.1
  143.2 0.7 copy.19
Async XLA Ops:
  138.3 3.6 %copy-start = (bf16[16,12,24,128]{3,2,1,0:T(8,128)(2,1)S(1)}, bf16[16,12,24,128]{3,2,1,0:T(8,128)(2,1)}, u32[]{:S(2)}) copy-start(bf16[16,12,24,128]{3,2,1,0:T(8,128)(2,1)} %get-tuple-element.9) | copy-start | bytes 3538948
  141.9 1.3 copy-start.1

commit v6 on v5

--- a/solution.py
+++ b/solution.py
@@ -147,7 +147,7 @@
 
 def layer_kernel(
     heads, valid_ref, pair_ref, cot_ref, gain_ref, bwt_ref, proj_ref,
-    atto_ref, pgo_ref, sums_ref, small_ref,
+    atto_ref, pgo_ref, sums_ref, small_ref, gain_out_ref,
     pair_f, cot_f, x_s, btile, x_hat_s, normed_s, w_in, xc, ball, bias_s, dbias_s, parts_s, gain_s,
     back_s, back, bterm,
     rbuf, psend, prbuf, zsend, zmate, zown, zback, zopp, parts_c, qr, qs, qp, qzs, qmate, qhalf, qopp, plane_g, outer_g,
@@ -470,7 +470,10 @@
     lax.fori_loop(ncols // 3, ncols, arrive_and_finish, 0)
     for i in range(n_out - 1):
         both(outer_g.at[0], s_small2.at[i], r_small2.at[i])
-    small_ref[...] = jnp.sum(outer_g[...], axis=0)
+    small = jnp.sum(outer_g[...], axis=0)
+    tall = jnp.transpose(jnp.concatenate([small, jnp.zeros((channels - 8, channels), F32)], axis=0))
+    small_ref[...] = tall[:, :heads]
+    gain_out_ref[...] = small[heads : heads + 1]
     both(sums_ref.at[core], s_agc, r_agc)
     await_bytes(x_s.at[pl.ds(0, n_row - 1)], s_fw)
     await_bytes(x_s.at[pl.ds(0, n_row - 1)], s_bw)
@@ -495,12 +498,13 @@
     return pl.pallas_call(
         functools.partial(layer_kernel, heads),
         in_specs=[pl.BlockSpec(memory_space=pltpu.SMEM)] + [vmem] * 5,
-        out_specs=[vmem] * 4,
+        out_specs=[vmem] * 5,
         out_shape=[
             jax.ShapeDtypeStruct(peers, BF16),
             jax.ShapeDtypeStruct(peers, F32),
             jax.ShapeDtypeStruct((2, 2, n_col) + slab, F32),
-            jax.ShapeDtypeStruct((8, channels), F32),
+            jax.ShapeDtypeStruct((channels, heads), F32),
+            jax.ShapeDtypeStruct((1, channels), F32),
         ],
         scratch_shapes=[
             flat, flat, VM((n_row, ncols, 2, tile_rows, channels), BF16),
@@ -553,15 +557,15 @@
         return jnp.swapaxes(columns.reshape(tile_cols, tile_rows, channels), 0, 1)
 
     bias_rows = jnp.pad(bias_weight.T, ((0, 8 - heads), (0, 0)))
-    attended, pair_gradient, sums, small = layer(
+    attended, pair_gradient, sums, bias_weight_grad, gain_gradient = layer(
         heads, valid_len, pair, out_cotangent, gain[None], bias_rows, projections
     )
     return (
         to_tile(attended),
         to_tile(pair_gradient),
         sums.reshape(5, channels, channels),
-        small[:heads].T,
-        small[heads],
+        bias_weight_grad,
+        gain_gradient[0],
     )
 
 

time: 144 us -> 142 us (0.986)
  local copies, waits for them, and re-layouts: 9.34 us -> 7.69 us
where the time goes in v6:
time: 142 us
  Pallas kernels  133 us (94%)
  local copies, waits for them, and re-layouts  7.69 us (5%)
    pallas_call x1, Pallas kernels, layer(): pl.pallas_call(functools.partial(layer_kernel, heads), in_specs=[pl.Block...  133 us
    reshape x2, local copies, waits for them, and re-layouts, to_tile(): return jnp.swapaxes(columns.reshape(tile_cols, tile_rows, channels), 0, 1)  4.52 us

profile of v6, /device:TPU:0, one launch (start us, length us, event | category | flops | bytes accessed | tf_op | source)
XLA Modules:
  0.0 142.3 jit_solution(6913010582484708017)
XLA Ops:
  1.3 1.3 pad.4.bwt_ref
  2.5 133.3 %shard_map.101 = (bf16[16,12,24,128]{3,2,1,0:T(8,128)(2,1)}, f32[16,12,24,128]{3,2,1,0:T(8,128)}, f32[2,2,2,80,128]{4,3,2,1,0:T(8,128)}, f32[128,4]{1,0:T(8,128)}, f32[1,128]{1,0:T(1,128)}) custom-call(s32[1]{0:T(128)S(6)} %copy.20.valid_ref, bf16[24,192,128]{2,1,0:T(8,128)(2,1)} %pair_ref.1, bf16[24,192,128]{2,1,0:T(8,128)(2,1)} %cot_ref.1, ...), custom_call_target="tpu_custom_call" | custom-call | tf_op jit(solution)/shard_map/pallas_call | solution.py:498
  135.9 0.0 copy-start
  135.9 2.7 %copy.17 = bf16[192,24,128]{2,0,1:T(8,128)(2,1)} copy(bf16[192,24,128]{2,1,0:T(8,128)(2,1)} %bitcast.15) | data formatting | bytes 2359296 | tf_op jit(solution)/shard_map/reshape | solution.py:557
  138.6 0.0 copy-done
  138.6 0.0 copy-start.2
  138.6 0.0 copy-start.1
  138.6 0.0 copy-start.3
  138.6 1.8 %copy.16 = f32[192,24,128]{2,0,1:T(8,128)} copy(f32[192,24,128]{2,1,0:T(8,128)S(1)} %bitcast.13) | data formatting | bytes 4718592 | tf_op jit(solution)/shard_map/reshape | solution.py:557
  140.4 0.0 copy-done.2
  140.4 0.7 copy.13
  141.1 0.0 copy-done.1
  141.1 0.7 copy.21
  141.8 0.0 copy-done.3
  141.8 0.5 copy.22
Async XLA Ops:
  135.9 2.7 %copy-start = (f32[16,12,24,128]{3,2,1,0:T(8,128)S(1)}, f32[16,12,24,128]{3,2,1,0:T(8,128)}, u32[]{:S(2)}) copy-start(f32[16,12,24,128]{3,2,1,0:T(8,128)} %get-tuple-element.11) | copy-start | bytes 7077892
  138.6 1.8 %copy-start.2 = (f32[128,4]{1,0:T(8,128)S(1)}, f32[128,4]{1,0:T(8,128)}, u32[]{:S(2)}) copy-start(f32[128,4]{1,0:T(8,128)} %get-tuple-element.18) | copy-start | bytes 6148
  138.6 2.5 %copy-start.1 = (f32[2,2,2,80,128]{4,3,2,1,0:T(8,128)S(1)}, f32[2,2,2,80,128]{4,3,2,1,0:T(8,128)}, u32[]{:S(2)}) copy-start(f32[2,2,2,80,128]{4,3,2,1,0:T(8,128)} %get-tuple-element.12) | copy-start | bytes 983044
  138.6 3.2 %copy-start.3 = (f32[1,128]{1,0:T(1,128)S(1)}, f32[1,128]{1,0:T(1,128)}, u32[]{:S(2)}) copy-start(f32[1,128]{1,0:T(1,128)} %get-tuple-element.14) | copy-start | bytes 1540
